TPU v7x, 32 devices: a whole 2x2x4 slice. The times are simulated.
32 devices in a mesh: dp: 8 (over y, x, core), tensor: 4 (over z).
Axes of the slice: x: 2, y: 2, z: 4, core: 2. Of those that a mesh axis runs over, the one named last changes fastest.
Arguments:
- inputs: bfloat16 [384, 200704], P('tensor', 'dp'), may hold values from -6 to 6
- crop_size: int32 [256, 4, 2], P('dp'), may hold values from 6 to 14, as said below
- crop_offset: int32 [256, 4, 2], P('dp'), may hold values from 0 to 8, as said below
- a_log: float32 [384, 64], P('tensor'), may hold values from -1.5 to 0.5
- a_imag: float32 [384, 64], P('tensor'), may hold values from 0 to 6
- c_height: float32 [2, 384, 64], P(None, 'tensor'), may hold values from -0.36 to 0.36
- c_width: float32 [2, 384, 64], P(None, 'tensor'), may hold values from -0.36 to 0.36
- log_dt: float32 [2, 384], P(None, 'tensor'), may hold values from -3 to -0.7
- skip_gain: float32 [384], P('tensor'), may hold values from 0.5 to 1.5
- ln_gain: float32 [384], replicated, may hold values from 0.1 to 1.9
- ln_bias: float32 [384], replicated, may hold values from -1.8 to 1.8
- w_in: bfloat16 [384, 1536], P(None, 'tensor'), may hold values from -0.3125 to 0.3125
- b_in: float32 [1536], P('tensor'), may hold values from -1.8 to 1.8
- w_out: bfloat16 [1536, 384], P('tensor'), may hold values from -0.15625 to 0.15625
- b_out: float32 [384], replicated, may hold values from -1.8 to 1.8
- layer_scale: float32 [384], replicated, may hold values from 0.5 to 2
- grad_out: bfloat16 [384, 200704], P('tensor', 'dp'), may hold values from -6 to 6
Outputs:
- result: bfloat16 [384, 200704], P('tensor', 'dp')
- grad_inputs: float32 [384, 200704], P('tensor', 'dp')
- grad_a_log: float32 [384, 64], P('tensor')
- grad_a_imag: float32 [384, 64], P('tensor')
- grad_c_height: float32 [2, 384, 64], P(None, 'tensor')
- grad_c_width: float32 [2, 384, 64], P(None, 'tensor')
- grad_log_dt: float32 [2, 384], P(None, 'tensor')
- grad_skip_gain: float32 [384], P('tensor')
- grad_ln_gain: float32 [384], P('tensor')
- grad_ln_bias: float32 [384], P('tensor')
- grad_w_in: float32 [384, 1536], P(None, 'tensor')
- grad_b_in: float32 [1536], P('tensor')
- grad_w_out: float32 [1536, 384], P('tensor')
- grad_b_out: float32 [384], P('tensor')
- grad_layer_scale: float32 [384], P('tensor')
Inputs may be any that keep to these rules, and one draw needn't show every extreme that they name: `crop_size`: each crop fits its slot (offset plus size at most 14); in every canvas one slot, drawn from the seed, holds a full 14 x 14 crop, and another holds a crop of the least size. `crop_offset`: offsets with crop_size give crops inside their slots.
All inputs are finite; a program needn't handle non-finite values.
Results may differ from a plain program's by a relative error of at most 0.0071.
Values may be sent and summed in bfloat16 or wider, within the bound.
A program may use at most 448 MiB of HBM per device.

v0:
```python
import jax
import jax.numpy as jnp
from jax import lax
from jax.sharding import PartitionSpec as P

CROP = 14


EPS = 1e-06


def crop_mask(crop_size, crop_offset, crop_len):
    canvases = crop_size.shape[0]
    spot_idx = jnp.arange(crop_len, dtype=jnp.int32)
    extent = crop_size.reshape(canvases, 2, 2, 2)
    anchor = crop_offset.reshape(canvases, 2, 2, 2)
    row_in = (spot_idx >= anchor[..., 0:1]) & (spot_idx < anchor[..., 0:1] + extent[..., 0:1])
    col_in = (spot_idx >= anchor[..., 1:2]) & (spot_idx < anchor[..., 1:2] + extent[..., 1:2])
    row_turned = jnp.transpose(row_in, (0, 1, 3, 2))
    return (row_turned[:, :, :, :, None] & col_in[:, :, None, :, :]).astype(jnp.float32)


def mixer_kernel(a_log, a_imag, c_pair, step_size, crop_len):
    lag_steps = jnp.arange(crop_len).astype(jnp.float32)
    decays = jnp.exp(-(step_size[:, None] * jnp.exp(a_log))[:, :, None] * lag_steps)
    phases = (step_size[:, None] * a_imag)[:, :, None] * lag_steps
    waves = c_pair[0][:, :, None] * jnp.cos(phases) - c_pair[1][:, :, None] * jnp.sin(phases)
    return jnp.sum(decays * waves, axis=1)


def toeplitz(kernel, crop_len):
    spot_idx = jnp.arange(crop_len, dtype=jnp.int32)
    lag_table = (
        spot_idx[:, None, None] == spot_idx[None, :, None] - spot_idx[None, None, :]
    ).astype(jnp.float32)
    return jnp.einsum("cl,lhk->chk", kernel, lag_table, precision=lax.Precision.HIGHEST)


def mixer_first(mixer_params, source, inside):
    a_log, a_imag, c_height, c_width, log_dt, skip_gain = mixer_params
    crop_len = source.shape[3]
    step_size = jnp.exp(log_dt)
    kern_height = toeplitz(mixer_kernel(a_log, a_imag, c_height, step_size[0], crop_len), crop_len)
    kern_width = toeplitz(mixer_kernel(a_log, a_imag, c_width, step_size[1], crop_len), crop_len)
    masked = inside[None] * source
    along_rows = jnp.einsum(
        "chk,cnakbw->cnahbw", kern_height, masked, precision=lax.Precision.HIGHEST
    )
    conv_out = jnp.einsum(
        "cwk,cnahbk->cnahbw", kern_width, along_rows, precision=lax.Precision.HIGHEST
    )
    return inside[None] * conv_out + skip_gain[:, None, None, None, None, None] * source


def per_device(
    inputs,
    crop_size,
    crop_offset,
    a_log,
    a_imag,
    c_height,
    c_width,
    log_dt,
    skip_gain,
    ln_gain,
    ln_bias,
    w_in,
    b_in,
    w_out,
    b_out,
    layer_scale,
    grad_out,
):
    local_width, pixels = inputs.shape
    canvases = crop_size.shape[0]
    crop_len = CROP
    start_col = lax.axis_index("tensor") * local_width
    inside = crop_mask(crop_size, crop_offset, crop_len)
    residual_in = inputs.astype(jnp.float32)
    source = residual_in.reshape(local_width, canvases, 2, crop_len, 2, crop_len)

    def local_mixer(params_in, source_in):
        return mixer_first(params_in, source_in, inside)

    mixed, mixer_back = jax.vjp(
        local_mixer, (a_log, a_imag, c_height, c_width, log_dt, skip_gain), source
    )
    mixed_low = mixed.reshape(local_width, pixels).astype(jnp.bfloat16)
    mixed_full = lax.all_gather(mixed_low, "tensor", axis=0, tiled=True).astype(jnp.float32)
    row_mean = jnp.mean(mixed_full, axis=0, keepdims=True)
    centered = mixed_full - row_mean
    row_scale = lax.rsqrt(jnp.mean(centered * centered, axis=0, keepdims=True) + EPS)
    normed = centered * row_scale
    normed_low = (normed * ln_gain[:, None] + ln_bias[:, None]).astype(jnp.bfloat16)
    pre_act = (
        lax.dot_general(
            w_in, normed_low, (((0,), (0,)), ((), ())), preferred_element_type=jnp.float32
        )
        + b_in[:, None]
    )
    activated, gelu_back = jax.vjp(jax.nn.gelu, pre_act)
    hidden = activated.astype(jnp.bfloat16)
    partial_out = lax.dot_general(
        w_out, hidden, (((0,), (0,)), ((), ())), preferred_element_type=jnp.float32
    )
    bias_local = lax.dynamic_slice_in_dim(b_out, start_col, local_width)
    branch = (
        lax.psum_scatter(partial_out, "tensor", scatter_dimension=0, tiled=True)
        + bias_local[:, None]
    )
    scale_local = lax.dynamic_slice_in_dim(layer_scale, start_col, local_width)
    result = (residual_in + scale_local[:, None] * branch).astype(jnp.bfloat16)
    grad_rows_local = grad_out.astype(jnp.float32)
    grad_scale = jnp.sum(grad_rows_local * branch, axis=1)
    grad_branch = (grad_rows_local * scale_local[:, None]).astype(jnp.bfloat16)
    grad_bout = jnp.sum(grad_branch.astype(jnp.float32), axis=1)
    grad_full = lax.all_gather(grad_branch, "tensor", axis=0, tiled=True)
    grad_wout = lax.dot_general(
        hidden, grad_full, (((1,), (1,)), ((), ())), preferred_element_type=jnp.float32
    )
    grad_hidden = lax.dot_general(
        w_out, grad_full, (((1,), (0,)), ((), ())), preferred_element_type=jnp.float32
    )
    grad_pre = gelu_back(grad_hidden)[0].astype(jnp.bfloat16)
    grad_bin = jnp.sum(grad_pre.astype(jnp.float32), axis=1)
    grad_win = lax.dot_general(
        normed_low, grad_pre, (((1,), (1,)), ((), ())), preferred_element_type=jnp.float32
    )
    grad_normed_part = lax.dot_general(
        w_in, grad_pre, (((1,), (0,)), ((), ())), preferred_element_type=jnp.float32
    )
    gain_local = lax.dynamic_slice_in_dim(ln_gain, start_col, local_width)
    normed_local = lax.dynamic_slice_in_dim(normed, start_col, local_width, 0)
    grad_normed = lax.psum(grad_normed_part, "tensor")
    grad_scaled = grad_normed * ln_gain[:, None]
    mean_one = jnp.mean(grad_scaled, axis=0, keepdims=True)
    mean_two = jnp.mean(grad_scaled * normed, axis=0, keepdims=True)
    grad_local = lax.dynamic_slice_in_dim(grad_normed, start_col, local_width, 0)
    grad_mixed = row_scale * (grad_local * gain_local[:, None] - mean_one - normed_local * mean_two)
    grad_gain = jnp.sum(grad_local * normed_local, axis=1)
    grad_lnbias = jnp.sum(grad_local, axis=1)
    param_grads, grad_source = mixer_back(grad_mixed.reshape(mixed.shape))
    grad_inputs = grad_rows_local + grad_source.reshape(local_width, pixels)
    summed = lax.psum(
        (
            param_grads[0],
            param_grads[1],
            param_grads[2],
            param_grads[3],
            param_grads[4],
            param_grads[5],
            grad_gain,
            grad_lnbias,
            grad_win,
            grad_bin,
            grad_wout,
            grad_bout,
            grad_scale,
        ),
        "dp",
    )
    return (
        result,
        grad_inputs,
        summed[0],
        summed[1],
        summed[2],
        summed[3],
        summed[4],
        summed[5],
        summed[6],
        summed[7],
        summed[8],
        summed[9],
        summed[10],
        summed[11],
        summed[12],
    )


def solution(mesh):
    in_specs = (
        P("tensor", "dp"),
        P("dp", None, None),
        P("dp", None, None),
        P("tensor", None),
        P("tensor", None),
        P(None, "tensor", None),
        P(None, "tensor", None),
        P(None, "tensor"),
        P("tensor"),
        P(),
        P(),
        P(None, "tensor"),
        P("tensor"),
        P("tensor", None),
        P(),
        P(),
        P("tensor", "dp"),
    )
    out_specs = (
        P("tensor", "dp"),
        P("tensor", "dp"),
        P("tensor", None),
        P("tensor", None),
        P(None, "tensor", None),
        P(None, "tensor", None),
        P(None, "tensor"),
        P("tensor"),
        P("tensor"),
        P("tensor"),
        P(None, "tensor"),
        P("tensor"),
        P("tensor", None),
        P("tensor"),
        P("tensor"),
    )
    return jax.shard_map(
        per_device, mesh=mesh, in_specs=in_specs, out_specs=out_specs, check_vma=False
    )
```

profile of v0, /device:TPU:24, one launch (start us, length us, event | category | flops | bytes accessed | tf_op | source)
XLA Modules:
  0.0 3644.5 jit_solution(11689021335111260451)
XLA Ops:
  50.1 27.3 copy.177
  78.1 47.4 %convolution_bitcast_fusion.3 = f32[96,32,2,14,2,14]{1,3,5,4,2,0:T(8,128)} fusion(f32[96,32,2,14,2,14]{1,3,5,4,2,0:T(8,128)} %copy.177, f32[96,14,14,1,1,1]{1,2,5,4,3,0:T(8,128)S(1)} %copy.210), kind=kOutput, calls=%fused_computation.40 | convolution fusion | flops 404619264 | bytes 19342848 | tf_op jit(solution)/shard_map/jvp(chk,cnakbw->cnahbw)/dot_general | solution.py:46
  125.5 69.4 %fusion.8 = f32[96,32,2,14,2,14]{1,5,4,3,2,0:T(8,128)} fusion(f32[96,14,14,1,1,1]{1,2,5,4,3,0:T(8,128)S(1)} %copy.209, f32[96,32,2,14,2,14]{1,3,5,4,2,0:T(8,128)} %convolution_bitcast_fusion.3), kind=kOutput, calls=%fused_computation.12 | convolution fusion | flops 404619264 | bytes 19342848 | tf_op jit(solution)/shard_map/jvp(cwk,cnahbk->cnahbw)/dot_general | solution.py:49
  194.9 29.2 copy.182
  224.1 14.2 add_convert_fusion.2
  263.5 327.6 %all-gather.3.cloned.1.call-done = bf16[384,25088]{1,0:T(8,128)(2,1)} async-done(((bf16[96,25088]{1,0:T(8,128)(2,1)}), bf16[384,25088]{1,0:T(8,128)(2,1)}) %all-gather.3.cloned.1.call-update) | async-done | bytes 19267600 | tf_op jit(solution)/shard_map/all_gather | solution.py:89
  591.1 25.8 copy.186
  628.4 16.8 fusion.10
  645.3 35.4 fusion.21
  680.8 22.2 convolution_bitcast_fusion.1
  703.0 38.3 %copy.225 = f32[384,25088]{1,0:T(8,128)} copy(f32[384,25088]{0,1:T(8,128)} %convolution_bitcast_fusion.1) | data formatting | bytes 77070336
  751.5 622.8 %reduce-scatter.4.cloned.1.call-done = f32[96,25088]{1,0:T(8,128)} async-done(((f32[384,25088]{1,0:T(8,128)}), f32[96,25088]{1,0:T(8,128)}) %reduce-scatter.4.cloned.1.call-update) | async-done | bytes 9633808
  1386.0 14.7 fusion.23
  1409.0 327.9 %all-gather.5.cloned.1.call-done = bf16[384,25088]{1,0:T(8,128)(2,1)} async-done(((bf16[96,25088]{1,0:T(8,128)(2,1)}), bf16[384,25088]{1,0:T(8,128)(2,1)}) %all-gather.5.cloned.1.call-update) | async-done | bytes 19267600 | tf_op jit(solution)/shard_map/all_gather | solution.py:117
  1736.9 42.4 %convert_reduce_fusion.1 = (f32[384]{0:T(512)}, bf16[384,25088]{0,1:T(8,128)(2,1)}) fusion(f32[25088,384]{1,0:T(8,128)} %get-tuple-element.159, bf16[384,25088]{1,0:T(8,128)(2,1)} %all-gather.5.cloned.1.call-done, bf16[384,384]{1,0:T(8,128)(2,1)S(1)} %copy-done.12), kind=kOutput, calls=%fused_computation.29 | convolution fusion | flops 7610695168 | bytes 77366784 | tf_op jit(solution)/shard_map/dot_general | solution.py:121
  1779.3 22.5 convolution_bitcast_fusion
  1810.4 18.2 fusion.86
  1828.6 28.0 fusion.25
  1856.7 1208.9 %all-reduce.12.cloned.1.call-done = f32[384,25088]{0,1:T(8,128)} async-done(((f32[384,25088]{0,1:T(8,128)}), f32[384,25088]{0,1:T(8,128)}) %all-reduce.12.cloned.1.call-update) | async-done | bytes 38535184 | tf_op jit(solution)/shard_map/psum | solution.py:134
  3065.6 32.8 multiply_reduce_fusion.1
  3098.5 22.3 dynamic-slice_reduce_fusion
  3120.7 14.9 reshape.193
  3148.9 27.5 copy.191
  3176.4 76.1 %fusion.26 = f32[96,14,14]{2,1,0:T(8,128)S(1)} fusion(f32[96,32,2,14,2,14]{1,5,4,3,2,0:T(8,128)} %copy.191, f32[96,32,2,14,2,14]{1,3,5,4,2,0:T(8,128)} %convolution_bitcast_fusion.3), kind=kOutput, calls=%fused_computation.55 | convolution fusion | flops 404619264 | bytes 19342848 | tf_op jit(solution)/shard_map/transpose(jvp(cwk,cnahbk->cnahbw))/dot_general | solution.py:49
  3252.5 47.5 %convolution_bitcast_fusion.2 = f32[96,32,2,2,14,14]{1,4,3,5,2,0:T(8,128)} fusion(f32[96,32,2,14,2,14]{1,5,4,3,2,0:T(8,128)} %copy.191, f32[96,14,14,1,1,1]{1,2,5,4,3,0:T(8,128)S(1)} %copy-done.5), kind=kOutput, calls=%fused_computation.39 | convolution fusion | flops 404619264 | bytes 19342848 | tf_op jit(solution)/shard_map/transpose(jvp(cwk,cnahbk->cnahbw))/dot_general | solution.py:49
  3300.0 88.8 %fusion.29 = f32[96,14,14]{2,1,0:T(8,128)S(1)} fusion(f32[96,32,2,14,2,14]{1,3,5,4,2,0:T(8,128)} %copy.177, f32[96,32,2,2,14,14]{1,4,3,5,2,0:T(8,128)} %convolution_bitcast_fusion.2), kind=kOutput, calls=%fused_computation.56 | convolution fusion | flops 404619264 | bytes 19342848 | tf_op jit(solution)/shard_map/transpose(jvp(chk,cnakbw->cnahbw))/dot_general | solution.py:46
  3388.9 82.1 %fusion.4 = f32[96,32,2,2,14,14]{1,5,4,3,2,0:T(8,128)} fusion(f32[96,14,14,1,1,1]{1,2,5,4,3,0:T(8,128)S(1)} %copy-done.7, f32[96,32,2,2,14,14]{1,4,3,5,2,0:T(8,128)} %convolution_bitcast_fusion.2), kind=kOutput, calls=%fused_computation.8 | convolution fusion | flops 404619264 | bytes 19342848 | tf_op jit(solution)/shard_map/transpose(jvp(chk,cnakbw->cnahbw))/dot_general | solution.py:46
  3472.5 30.4 copy.195
  3502.8 18.2 fusion.24
  3526.1 17.4 copy.196
  3543.5 14.9 reshape.194
  3582.5 37.0 %all-reduce.14.cloned.1.call-done = (f32[96,64]{0,1:T(8,128)}, f32[96,64]{0,1:T(8,128)}, f32[2,96,64]{1,2,0:T(8,128)}, f32[2,96,64]{1,2,0:T(8,128)}, f32[2,96]{1...) async-done(((f32[96,64]{0,1:T(8,128)}, f32[96,64]{0,1:T(8,128)}, f32[2,96,64]{1,2,0:T(8,128)}, ...) | async-done | bytes 151696 | tf_op jit(solution)/shard_map/psum | solution.py:144
  (179 shorter events, 180.3 us)
Async XLA Ops:
  7.2 638.0 %copy-start = (bf16[384,384]{1,0:T(8,128)(2,1)S(1)}, bf16[384,384]{1,0:T(8,128)(2,1)}, u32[]{:S(2)}) copy-start(bf16[384,384]{1,0:T(8,128)(2,1)} %param.28) | copy-start | bytes 884740
  7.2 583.9 %all-gather.3.cloned.1.call-start = ((), (), s32[]{:S(2)}) async-start(), calls=%async_computation.1 | async-start | bytes 24084480 | tf_op jit(solution)/shard_map/all_gather | solution.py:89
  7.3 70.1 %copy-start.13 = (s32[14,14]{1,0:T(8,128)}, s32[14,14]{1,0:T(8,128)S(1)}, u32[]{:S(2)}) copy-start(s32[14,14]{1,0:T(8,128)S(1)} %iota_subtract_fusion) | copy-start | bytes 2356
  15.0 63.1 %copy-start.6 = (f32[96,14,14,1,1,1]{1,2,5,4,3,0:T(8,128)}, f32[96,14,14,1,1,1]{1,2,5,4,3,0:T(8,128)S(1)}, u32[]{:S(2)}) copy-start(f32[96,14,14,1,1,1]{1,2,5,4,3,0:T(8,128)S(1)} %copy.210) | copy-start | bytes 225796
  36.7 187.5 %copy-start.2 = (f32[32,2,14,2,14]{0,4,3,2,1:T(8,128)}, f32[32,2,14,2,14]{0,4,3,2,1:T(8,128)S(1)}, u32[]{:S(2)}) copy-start(f32[32,2,14,2,14]{0,4,3,2,1:T(8,128)S(1)} %and_convert_fusion) | copy-start | bytes 301060
  263.4 381.8 %copy-start.38 = (f32[384]{0:T(512)S(1)}, f32[384]{0:T(512)}, u32[]{:S(2)}) copy-start(f32[384]{0:T(512)} %param.26) | copy-start | bytes 4612
  263.4 381.8 %copy-start.42 = (f32[384]{0:T(512)S(1)}, f32[384]{0:T(512)}, u32[]{:S(2)}) copy-start(f32[384]{0:T(512)} %param.29) | copy-start | bytes 4612
  263.4 381.8 %copy-start.43 = (f32[384]{0:T(512)S(1)}, f32[384]{0:T(512)}, u32[]{:S(2)}) copy-start(f32[384]{0:T(512)} %param.27) | copy-start | bytes 4612
  263.4 1110.9 %reduce-scatter.4.cloned.1.call-start = ((), (), s32[]{:S(2)}) async-start(), calls=%async_computation.4 | async-start | bytes 48168960
  628.4 52.4 %copy-start.10 = (f32[25088]{0:T(1024)}, f32[25088]{0:T(1024)S(1)}, u32[]{:S(2)}) copy-start(f32[25088]{0:T(1024)S(1)} %broadcast_multiply_fusion.2) | copy-start | bytes 301060
  741.3 995.7 %all-gather.5.cloned.1.call-start = ((), (), s32[]{:S(2)}) async-start(), calls=%async_computation.2 | async-start | bytes 24084480 | tf_op jit(solution)/shard_map/all_gather | solution.py:117
  1409.0 1656.7 %all-reduce.12.cloned.1.call-start = ((), (), s32[]{:S(2)}) async-start(), calls=%async_computation.3 | async-start | bytes 77070336 | tf_op jit(solution)/shard_map/psum | solution.py:134
  1801.9 1780.6 %all-reduce.16.cloned.1.call-start = ((), (), s32[]{:S(2)}) async-start(), calls=%async_computation.6 | async-start | bytes 2359296 | tf_op jit(solution)/shard_map/psum | solution.py:144
  1856.7 1762.9 %all-reduce.14.cloned.1.call-start = ((), (), s32[]{:S(2)}) async-start(), calls=%async_computation.5 | async-start | bytes 404480 | tf_op jit(solution)/shard_map/psum | solution.py:144
  3176.4 76.1 %copy-start.5 = (f32[96,14,14,1,1,1]{1,2,5,4,3,0:T(8,128)S(1)}, f32[96,14,14,1,1,1]{1,2,5,4,3,0:T(8,128)}, u32[]{:S(2)}) copy-start(f32[96,14,14,1,1,1]{1,2,5,4,3,0:T(8,128)} %copy-done.4) | copy-start | bytes 225796
  3300.0 88.8 %copy-start.7 = (f32[96,14,14,1,1,1]{1,2,5,4,3,0:T(8,128)S(1)}, f32[96,14,14,1,1,1]{1,2,5,4,3,0:T(8,128)}, u32[]{:S(2)}) copy-start(f32[96,14,14,1,1,1]{1,2,5,4,3,0:T(8,128)} %copy-done.6) | copy-start | bytes 225796
  3388.9 82.2 %copy-start.14 = (s32[14,14]{1,0:T(8,128)S(1)}, s32[14,14]{1,0:T(8,128)}, u32[]{:S(2)}) copy-start(s32[14,14]{1,0:T(8,128)} %copy-done.13) | copy-start | bytes 2356
  3472.3 48.8 %copy-start.18 = (f32[96,64]{0,1:T(8,128)S(1)}, f32[96,64]{0,1:T(8,128)}, u32[]{:S(2)}) copy-start(f32[96,64]{0,1:T(8,128)} %copy-done.17) | copy-start | bytes 73732
  3472.3 48.8 %copy-start.20 = (f32[96,64]{0,1:T(8,128)S(1)}, f32[96,64]{0,1:T(8,128)}, u32[]{:S(2)}) copy-start(f32[96,64]{0,1:T(8,128)} %copy-done.19) | copy-start | bytes 73732
  3472.3 48.7 %copy-start.22 = (f32[96,64]{0,1:T(8,128)S(1)}, f32[96,64]{0,1:T(8,128)}, u32[]{:S(2)}) copy-start(f32[96,64]{0,1:T(8,128)} %copy-done.21) | copy-start | bytes 73732
  3472.4 48.7 %copy-start.24 = (f32[96,64]{0,1:T(8,128)S(1)}, f32[96,64]{0,1:T(8,128)}, u32[]{:S(2)}) copy-start(f32[96,64]{0,1:T(8,128)} %copy-done.23) | copy-start | bytes 73732
  3472.4 48.7 %copy-start.26 = (f32[96,64]{0,1:T(8,128)S(1)}, f32[96,64]{0,1:T(8,128)}, u32[]{:S(2)}) copy-start(f32[96,64]{0,1:T(8,128)} %copy-done.25) | copy-start | bytes 73732
  3472.4 48.7 %copy-start.28 = (f32[96,64]{0,1:T(8,128)S(1)}, f32[96,64]{0,1:T(8,128)}, u32[]{:S(2)}) copy-start(f32[96,64]{0,1:T(8,128)} %copy-done.27) | copy-start | bytes 73732
  3472.4 48.7 %copy-start.30 = (f32[96,64]{0,1:T(8,128)S(1)}, f32[96,64]{0,1:T(8,128)}, u32[]{:S(2)}) copy-start(f32[96,64]{0,1:T(8,128)} %copy-done.29) | copy-start | bytes 73732
  3472.4 48.7 %copy-start.32 = (f32[96,64]{0,1:T(8,128)S(1)}, f32[96,64]{0,1:T(8,128)}, u32[]{:S(2)}) copy-start(f32[96,64]{0,1:T(8,128)} %copy-done.31) | copy-start | bytes 73732
  3472.4 48.7 %copy-start.46 = (f32[14]{0:T(128)S(1)}, f32[14]{0:T(128)}, u32[]{:S(2)}) copy-start(f32[14]{0:T(128)} %copy-done.45) | copy-start | bytes 172
  3472.4 52.9 %copy-start.15 = (f32[96,64]{0,1:T(8,128)S(1)}, f32[96,64]{0,1:T(8,128)}, u32[]{:S(2)}) copy-start(f32[96,64]{0,1:T(8,128)} %param.21) | copy-start | bytes 73732
  3472.4 52.9 %copy-start.16 = (f32[96,64]{0,1:T(8,128)S(1)}, f32[96,64]{0,1:T(8,128)}, u32[]{:S(2)}) copy-start(f32[96,64]{0,1:T(8,128)} %param.20) | copy-start | bytes 73732
  3472.4 52.9 %copy-start.34 = (f32[96]{0:T(128)S(1)}, f32[96]{0:T(128)}, u32[]{:S(2)}) copy-start(f32[96]{0:T(128)} %copy-done.33) | copy-start | bytes 1156
  3472.5 52.9 %copy-start.36 = (f32[96]{0:T(128)S(1)}, f32[96]{0:T(128)}, u32[]{:S(2)}) copy-start(f32[96]{0:T(128)} %copy-done.35) | copy-start | bytes 1156
  3502.8 56.3 %copy-start.37 = (f32[2,96]{1,0:T(2,128)S(1)}, f32[2,96]{1,0:T(2,128)}, u32[]{:S(2)}) copy-start(f32[2,96]{1,0:T(2,128)} %param.24) | copy-start | bytes 2308
  3526.1 111.3 %copy-start.1 = (bf16[384,384]{1,0:T(8,128)(2,1)S(1)}, bf16[384,384]{1,0:T(8,128)(2,1)}, u32[]{:S(2)}) copy-start(bf16[384,384]{1,0:T(8,128)(2,1)} %param.28) | copy-start | bytes 884740
  (26 other events, 515.2 us)
Sparse Core Ops, SparseCore 0:
  263.5 327.5 all-gather.2
  741.4 632.9 reduce-scatter.3
  1409.1 327.7 all-gather.4
  1802.0 1263.6 all-reduce.11
  3069.3 59.2 all-reduce.15
  3559.8 59.6 all-reduce.13
where the time goes:
time: 3660 us; the launch traced here: 3640 us
  waiting for transfers between devices  2520 us (69%)
  matrix products  582 us (16%)
  local copies, waits for them, and re-layouts  344 us (9%)
  other arithmetic  179 us (5%)
    psum x1, waiting for transfers between devices, per_device(): grad_normed = lax.psum(grad_normed_part, 'tensor')  1210 us
    unnamed x7, waiting for transfers between devices  623 us
    all_gather x1, waiting for transfers between devices, per_device(): grad_full = lax.all_gather(grad_branch, 'tensor', axis=0, tiled=True)  328 us
    all_gather x1, waiting for transfers between devices, per_device(): lax.all_gather(mixed_low, 'tensor', axis=0, tiled=True).astype(jnp.float32)  328 us
    dot_general x3, matrix products, mixer_first(): jnp.einsum('chk,cnakbw->cnahbw', kern_height, masked, precision=lax.Preci...  218 us
    dot_general x3, matrix products, mixer_first(): jnp.einsum('cwk,cnahbk->cnahbw', kern_width, along_rows, precision=lax.Pr...  193 us
    unnamed x123, local copies, waits for them, and re-layouts  105 us
  transfers between devices with their start and end apart: 6, of which 5 were waited for; matrix products, arithmetic and copies ran while one was open for 16% of the time, Pallas kernels for 0%

commit v1 on v0

v1 whole, which is shorter than its diff:
```python
import functools

import jax
import jax.numpy as jnp
from jax import lax
from jax.experimental import pallas as pl
from jax.experimental.pallas import tpu as pltpu
from jax.sharding import PartitionSpec as P

F32, BF16 = jnp.float32, jnp.bfloat16
CROP = 14
SIDE = 2 * CROP
NPIX = SIDE * SIDE
LANES = 128
GROUP = 32
STEP = 896
FTILE = 256
EPS = 1e-06
GELU_C = 0.7978845608028654
GELU_A = 0.044715
VMEM = 60 << 20


def nn(a, b):
    return lax.dot_general(a, b, (((1,), (0,)), ((), ())), preferred_element_type=F32)


def nt(a, b):
    return lax.dot_general(a, b, (((1,), (1,)), ((), ())), preferred_element_type=F32)


def lanes_to_rows(load, rows):
    @pl.loop(0, rows.shape[0] // STEP)
    def _(j):
        off = pl.multiple_of(j * STEP, LANES)
        rows[pl.ds(off, STEP), :] = jnp.transpose(load(off).astype(F32))


def rows_to_lanes(rows, store):
    @pl.loop(0, rows.shape[0] // STEP)
    def _(j):
        off = pl.multiple_of(j * STEP, LANES)
        store(off, jnp.transpose(rows[pl.ds(off, STEP), :]).astype(BF16))


def conv(y, taps):
    return [sum((taps[l] * y[i - l] for l in range(1, i + 1)), taps[0] * y[i]) for i in range(CROP)]


def conv_back(y, taps):
    return [
        sum((taps[l] * y[i + l] for l in range(1, CROP - i)), taps[0] * y[i]) for i in range(CROP)
    ]


def tap_rows(kern_ref, base):
    return [jnp.broadcast_to(kern_ref[pl.ds(base + l, 1), :], (8, LANES)) for l in range(CROP)]


def spot(slot, h, w):
    first = (slot // 2) * (CROP * SIDE) + (slot % 2) * CROP
    return pl.ds(first + h * SIDE + w, 8, stride=NPIX)


def mix_fwd_kernel(x_ref, kern_ref, mask_ref, out_ref, rows, inner):
    lanes_to_rows(lambda o: x_ref[:, 0, :, pl.ds(o, STEP)].reshape(LANES, STEP), rows)
    skip = jnp.broadcast_to(kern_ref[pl.ds(2 * CROP, 1), :], (8, LANES))

    @pl.loop(0, 4)
    def _(slot):
        @pl.loop(0, CROP)
        def _(h):
            taps = tap_rows(kern_ref, CROP)
            row_in = mask_ref[slot, h]
            y = [rows[spot(slot, h, w), :] * mask_ref[slot, CROP + w] for w in range(CROP)]
            for w, v in enumerate(conv(y, taps)):
                inner[h, w] = v * row_in

        @pl.loop(0, CROP)
        def _(w):
            taps = tap_rows(kern_ref, 0)
            col_in = mask_ref[slot, CROP + w]
            y = [inner[h, w] for h in range(CROP)]
            for h, v in enumerate(conv(y, taps)):
                at = spot(slot, h, w)
                rows[at, :] = v * (mask_ref[slot, h] * col_in) + skip * rows[at, :]

    def store(off, v):
        out_ref[:, 0, :, pl.ds(off, STEP)] = v.reshape(4, GROUP, STEP)

    rows_to_lanes(rows, store)


def mix_fwd(x4, kern, mask):
    pix = x4.shape[3]
    tile = pl.BlockSpec((4, 1, GROUP, pix), lambda q: (0, q, 0, 0))
    return pl.pallas_call(
        mix_fwd_kernel,
        grid=(x4.shape[1],),
        out_shape=jax.ShapeDtypeStruct(x4.shape, BF16),
        in_specs=[
            tile,
            pl.BlockSpec((32, LANES), lambda q: (0, q)),
            pl.BlockSpec(mask.shape, lambda q: (0, 0, 0, 0)),
        ],
        out_specs=tile,
        scratch_shapes=[pltpu.VMEM((pix, LANES), F32), pltpu.VMEM((CROP, CROP, 8, LANES), F32)],
        compiler_params=pltpu.CompilerParams(vmem_limit_bytes=VMEM),
        cost_estimate=pl.CostEstimate(flops=25 * 10**9, bytes_accessed=10**7, transcendentals=0),
        name="mix_fwd",
    )(x4, kern, mask)


def mix_bwd_kernel(x_ref, g_ref, kern_ref, mask_ref, out_ref, gk_ref, rows, grow, inner, mid):
    lanes_to_rows(lambda o: x_ref[:, 0, :, pl.ds(o, STEP)].reshape(LANES, STEP), rows)
    lanes_to_rows(lambda o: g_ref[:, 0, :, pl.ds(o, STEP)].reshape(LANES, STEP), grow)
    skip = jnp.broadcast_to(kern_ref[pl.ds(2 * CROP, 1), :], (8, LANES))
    zero = jnp.zeros((8, LANES), F32)

    def per_slot(slot, sums):
        gk_height, gk_width, gskip = sums

        @pl.loop(0, CROP)
        def _(h):
            taps = tap_rows(kern_ref, CROP)
            row_in = mask_ref[slot, h]
            y = [rows[spot(slot, h, w), :] * mask_ref[slot, CROP + w] for w in range(CROP)]
            for w, v in enumerate(conv(y, taps)):
                inner[h, w] = v * row_in

        def down(w, acc):
            taps = tap_rows(kern_ref, 0)
            col_in = mask_ref[slot, CROP + w]
            u = [grow[spot(slot, h, w), :] * (mask_ref[slot, h] * col_in) for h in range(CROP)]
            for h, v in enumerate(conv_back(u, taps)):
                mid[h, w] = v * mask_ref[slot, h]
            a = [inner[h, w] for h in range(CROP)]
            return tuple(
                sum((u[h] * a[h - l] for h in range(l, CROP)), acc[l]) for l in range(CROP)
            )

        gk_height = lax.fori_loop(0, CROP, down, gk_height)

        def across(h, acc):
            gk_width, gskip = acc
            taps = tap_rows(kern_ref, CROP)
            u = [mid[h, w] for w in range(CROP)]
            x = [rows[spot(slot, h, w), :] for w in range(CROP)]
            y = [x[w] * mask_ref[slot, CROP + w] for w in range(CROP)]
            gk_width = tuple(
                sum((u[w] * y[w - l] for w in range(l, CROP)), gk_width[l]) for l in range(CROP)
            )
            for w, v in enumerate(conv_back(u, taps)):
                at = spot(slot, h, w)
                g = grow[at, :]
                gskip = gskip + g * x[w]
                grow[at, :] = v * mask_ref[slot, CROP + w] + skip * g
            return gk_width, gskip

        gk_width, gskip = lax.fori_loop(0, CROP, across, (gk_width, gskip))
        return gk_height, gk_width, gskip

    gk_height, gk_width, gskip = lax.fori_loop(
        0, 4, per_slot, ((zero,) * CROP, (zero,) * CROP, zero)
    )
    gk_ref[...] = jnp.zeros_like(gk_ref)
    for row, v in enumerate((*gk_height, *gk_width, gskip)):
        gk_ref[pl.ds(row, 1), :] = jnp.sum(v, axis=0, keepdims=True)

    def store(off, v):
        out_ref[:, :, pl.ds(off, STEP)] = v.reshape(4, GROUP, STEP)

    rows_to_lanes(grow, store)


def mix_bwd(x4, g4, kern, mask, q):
    pix = x4.shape[3]
    tile = pl.BlockSpec((4, 1, GROUP, pix), lambda i: (0, q, 0, 0))
    return pl.pallas_call(
        mix_bwd_kernel,
        grid=(1,),
        out_shape=(
            jax.ShapeDtypeStruct((4, GROUP, pix), BF16),
            jax.ShapeDtypeStruct((32, LANES), F32),
        ),
        in_specs=[
            tile,
            tile,
            pl.BlockSpec((32, LANES), lambda i: (0, q)),
            pl.BlockSpec(mask.shape, lambda i: (0, 0, 0, 0)),
        ],
        out_specs=(
            pl.BlockSpec((4, GROUP, pix), lambda i: (0, 0, 0)),
            pl.BlockSpec((32, LANES), lambda i: (0, 0)),
        ),
        scratch_shapes=[pltpu.VMEM((pix, LANES), F32)] * 2
        + [pltpu.VMEM((CROP, CROP, 8, LANES), F32)] * 2,
        compiler_params=pltpu.CompilerParams(vmem_limit_bytes=VMEM),
        cost_estimate=pl.CostEstimate(flops=20 * 10**9, bytes_accessed=10**7, transcendentals=0),
        name="mix_bwd",
    )(x4, g4, kern, mask)


def norm(m):
    centered = m - jnp.mean(m, axis=0, keepdims=True)
    scale = lax.rsqrt(jnp.mean(centered * centered, axis=0, keepdims=True) + EPS)
    return centered * scale, scale


def ff_fwd_kernel(mix_ref, x_ref, win_t, wout_t, chan_ref, bin_ref, res_ref, hid_ref, slope_ref):
    normed, _ = norm(mix_ref[...].astype(F32))
    low = (normed * chan_ref[:, 0:1] + chan_ref[:, 1:2]).astype(BF16)
    for t in range(win_t.shape[0] // FTILE):
        sl = pl.ds(t * FTILE, FTILE)
        pre = nn(win_t[sl, :], low) + bin_ref[sl, 0:1]
        square = pre * pre
        th = jnp.tanh(pre * (GELU_C + (GELU_C * GELU_A) * square))
        half = 0.5 * th + 0.5
        hid_ref[sl, :] = (pre * half).astype(BF16)
        inner_slope = GELU_C + (3 * GELU_C * GELU_A) * square
        slope_ref[sl, :] = (half + pre * (0.5 - 0.5 * th * th) * inner_slope).astype(BF16)
    branch = nn(wout_t[...], hid_ref[...]) + chan_ref[:, 2:3]
    res_ref[...] = (x_ref[...].astype(F32) + chan_ref[:, 3:4] * branch).astype(BF16)


def lane_block(rows):
    return pl.BlockSpec((rows, STEP), lambda i: (0, i))


def whole(a):
    return pl.BlockSpec(a.shape, lambda i: (0,) * len(a.shape))


def ff_fwd(mix, x, win_t, wout_t, chan, bin_):
    width, pix = mix.shape
    ff = win_t.shape[0]
    return pl.pallas_call(
        ff_fwd_kernel,
        grid=(pix // STEP,),
        out_shape=(
            jax.ShapeDtypeStruct((width, pix), BF16),
            jax.ShapeDtypeStruct((ff, pix), BF16),
            jax.ShapeDtypeStruct((ff, pix), BF16),
        ),
        in_specs=[lane_block(width), lane_block(width)]
        + [whole(a) for a in (win_t, wout_t, chan, bin_)],
        out_specs=(lane_block(width), lane_block(ff), lane_block(ff)),
        compiler_params=pltpu.CompilerParams(vmem_limit_bytes=VMEM),
        cost_estimate=pl.CostEstimate(
            flops=4 * width * ff * pix, bytes_accessed=6 * 10**7, transcendentals=ff * pix
        ),
        name="ff_fwd",
    )(mix, x, win_t, wout_t, chan, bin_)


def fold(v):
    return sum(
        (v[:, i * LANES : (i + 1) * LANES] for i in range(1, v.shape[1] // LANES)), v[:, :LANES]
    )


def ff_bwd_kernel(
    go_ref, mix_ref, hid_ref, slope_ref, win, wout, chan_ref, gm_ref, dwo, dwi, bin_ref, vec_ref, gp
):
    @pl.when(pl.program_id(0) == 0)
    def _():
        for ref in (dwo, dwi, bin_ref, vec_ref):
            ref[...] = jnp.zeros_like(ref)

    go = go_ref[...].astype(F32)
    gb = (go * chan_ref[:, 3:4]).astype(BF16)
    vec_ref[0] += fold(gb.astype(F32))
    vec_ref[3] += fold(go)
    normed, scale = norm(mix_ref[...].astype(F32))
    low = (normed * chan_ref[:, 0:1] + chan_ref[:, 1:2]).astype(BF16)
    for t in range(wout.shape[0] // FTILE):
        sl = pl.ds(t * FTILE, FTILE)
        tile = (nn(wout[sl, :], gb) * slope_ref[sl, :].astype(F32)).astype(BF16)
        gp[sl, :] = tile
        bin_ref[sl, :] += fold(tile.astype(F32))
        dwo[sl, :] += nt(hid_ref[sl, :], gb)
        dwi[sl, :] += nt(tile, low)
    gn = nn(win[...], gp[...])
    vec_ref[1] += fold(gn * normed)
    vec_ref[2] += fold(gn)
    g1 = gn * chan_ref[:, 0:1]
    m1 = jnp.mean(g1, axis=0, keepdims=True)
    m2 = jnp.mean(g1 * normed, axis=0, keepdims=True)
    gm_ref[...] = scale * (g1 - m1 - normed * m2)


def ff_bwd(go, mix, hid, slope, win, wout, chan):
    width, pix = mix.shape
    ff = wout.shape[0]
    shapes = (
        jax.ShapeDtypeStruct((width, pix), F32),
        jax.ShapeDtypeStruct((ff, width), F32),
        jax.ShapeDtypeStruct((ff, width), F32),
        jax.ShapeDtypeStruct((ff, LANES), F32),
        jax.ShapeDtypeStruct((4, width, LANES), F32),
    )
    return pl.pallas_call(
        ff_bwd_kernel,
        grid=(pix // STEP,),
        out_shape=shapes,
        in_specs=[lane_block(width), lane_block(width), lane_block(ff), lane_block(ff)]
        + [whole(a) for a in (win, wout, chan)],
        out_specs=(lane_block(width),) + tuple(whole(s) for s in shapes[1:]),
        scratch_shapes=[pltpu.VMEM((ff, STEP), BF16)],
        compiler_params=pltpu.CompilerParams(vmem_limit_bytes=VMEM),
        cost_estimate=pl.CostEstimate(
            flops=8 * width * ff * pix, bytes_accessed=7 * 10**7, transcendentals=0
        ),
        name="ff_bwd",
    )(go, mix, hid, slope, win, wout, chan)


def finish_kernel(g_ref, go_ref, *rest):
    rest[-1][...] = go_ref[...].astype(F32) + g_ref[0].astype(F32)


def finish(g, grad_out, q, earlier):
    parts, rows, pix = g.shape
    tile = pl.BlockSpec((rows, pix), lambda s: (q, s))
    operands = (g, grad_out) if earlier is None else (g, grad_out, earlier)
    return pl.pallas_call(
        finish_kernel,
        grid=(parts,),
        out_shape=jax.ShapeDtypeStruct(grad_out.shape, F32),
        in_specs=[pl.BlockSpec((1, rows, pix), lambda s: (s, 0, 0)), tile]
        + [pl.BlockSpec(memory_space=pl.ANY)] * (earlier is not None),
        out_specs=tile,
        input_output_aliases={} if earlier is None else {2: 0},
        compiler_params=pltpu.CompilerParams(vmem_limit_bytes=32 << 20),
        name="finish",
    )(*operands)


def lag_kernels(a_log, a_imag, c_height, c_width, log_dt):
    step = jnp.exp(log_dt)[:, None, :, None]
    lags = jnp.arange(CROP, dtype=F32)[None, :, None, None]
    decays = jnp.exp(-(step * jnp.exp(a_log)[None, None]) * lags)
    phases = step * a_imag[None, None] * lags
    coef = jnp.stack([c_height, c_width])
    waves = coef[:, 0][:, None] * jnp.cos(phases) - coef[:, 1][:, None] * jnp.sin(phases)
    return jnp.sum(decays * waves, axis=3)


def slot_mask(crop_size, crop_offset):
    spots = jnp.arange(CROP, dtype=jnp.int32)
    low = crop_offset[..., None]
    inside = (spots >= low) & (spots < low + crop_size[..., None])
    inside = jnp.transpose(inside, (1, 2, 3, 0)).reshape(4, 2 * CROP, crop_size.shape[0])
    return jnp.broadcast_to(inside.astype(F32)[..., None], (*inside.shape, LANES))


def per_device(
    parts,
    groups,
    inputs,
    crop_size,
    crop_offset,
    a_log,
    a_imag,
    c_height,
    c_width,
    log_dt,
    skip_gain,
    ln_gain,
    ln_bias,
    w_in,
    b_in,
    w_out,
    b_out,
    layer_scale,
    grad_out,
):
    local, pixels = inputs.shape
    pix = pixels // parts
    width = local * parts
    tiles = local // GROUP
    me = lax.axis_index("tensor")

    def exchange(a):
        return lax.all_to_all(a, "tensor", 0, 0, tiled=True)

    def by_owner(a):
        return jnp.transpose(a.reshape(local, parts, pix), (1, 0, 2))

    x_all = exchange(by_owner(inputs))
    x_all, late = lax.optimization_barrier((x_all, grad_out))
    go_all = exchange(by_owner(late))

    lag, lag_back = jax.vjp(lag_kernels, a_log, a_imag, c_height, c_width, log_dt)
    kern = jnp.concatenate(
        [lag.reshape(2 * CROP, local), skip_gain[None], jnp.zeros((3, local), F32)]
    )
    kern = lax.all_gather(kern, "tensor")
    kern = jnp.transpose(kern.reshape(parts, 32, tiles, GROUP), (1, 2, 0, 3)).reshape(32, width)
    mine = crop_size.shape[0] // parts
    mask = slot_mask(
        lax.dynamic_slice_in_dim(crop_size, me * mine, mine),
        lax.dynamic_slice_in_dim(crop_offset, me * mine, mine),
    )
    win_t = lax.all_gather(jnp.transpose(w_in), "tensor", axis=0, tiled=True)
    wout = lax.all_gather(w_out, "tensor", axis=0, tiled=True)
    bin_ = lax.all_gather(b_in, "tensor", axis=0, tiled=True)
    ff = bin_.shape[0]
    chan = jnp.pad(jnp.stack([ln_gain, ln_bias, b_out, layer_scale], 1), ((0, 0), (0, LANES - 4)))

    x4 = x_all.reshape(parts, tiles, GROUP, pix)
    mixed = mix_fwd(x4, kern, mask).reshape(width, pix)
    res, hid, slope = ff_fwd(
        mixed,
        x_all.reshape(width, pix),
        win_t,
        jnp.transpose(wout),
        chan,
        jnp.broadcast_to(bin_[:, None], (ff, LANES)),
    )
    go_all, res = lax.optimization_barrier((go_all, res))
    res_own = exchange(res.reshape(parts, local, pix))
    gm, dwo, dwi, g_bin, vec = ff_bwd(
        go_all.reshape(width, pix), mixed, hid, slope, jnp.transpose(win_t), wout, chan
    )
    g4 = gm.reshape(parts, tiles, GROUP, pix)
    grad_inputs, gk = None, []
    for q in range(tiles):
        gx, gk_q = mix_bwd(x4, g4, kern, mask, q)
        gk.append(gk_q)
        grad_inputs = finish(exchange(gx), grad_out, q, grad_inputs)
    result = jnp.transpose(res_own, (1, 0, 2)).reshape(local, pixels)

    rows = ff // parts // groups
    dw = jnp.stack([dwo, dwi]).reshape(2, parts, groups, rows, width)
    dw = lax.psum_scatter(dw, "dp", scatter_dimension=2)
    dw = lax.psum_scatter(dw, "tensor", scatter_dimension=1)
    dw = lax.all_gather(dw, "dp", axis=1, tiled=True)

    vec = jnp.sum(vec, axis=2)
    g_scale = jnp.sum(dwo * wout.astype(F32), axis=0) / layer_scale + b_out * vec[3]
    vec = vec.at[3].set(g_scale)
    gk = jnp.stack(gk)
    vec, g_bin, gk = lax.psum((vec, jnp.sum(g_bin, axis=1), gk), ("dp", "tensor"))
    vec = lax.dynamic_slice_in_dim(vec, me * local, local, 1)
    g_bin = lax.dynamic_slice_in_dim(g_bin, me * b_in.shape[0], b_in.shape[0])
    gk = lax.dynamic_slice_in_dim(gk, me * GROUP, GROUP, 2)
    gk = jnp.transpose(gk, (1, 0, 2)).reshape(32, local)
    lag_grads = lag_back(gk[: 2 * CROP].reshape(2, CROP, local))
    return (
        result,
        grad_inputs,
        lag_grads[0],
        lag_grads[1],
        lag_grads[2],
        lag_grads[3],
        lag_grads[4],
        gk[2 * CROP],
        vec[1],
        vec[2],
        jnp.transpose(dw[1]),
        g_bin,
        dw[0],
        vec[0],
        vec[3],
    )


def solution(mesh):
    in_specs = (
        P("tensor", "dp"),
        P("dp", None, None),
        P("dp", None, None),
        P("tensor", None),
        P("tensor", None),
        P(None, "tensor", None),
        P(None, "tensor", None),
        P(None, "tensor"),
        P("tensor"),
        P(),
        P(),
        P(None, "tensor"),
        P("tensor"),
        P("tensor", None),
        P(),
        P(),
        P("tensor", "dp"),
    )
    out_specs = (
        P("tensor", "dp"),
        P("tensor", "dp"),
        P("tensor", None),
        P("tensor", None),
        P(None, "tensor", None),
        P(None, "tensor", None),
        P(None, "tensor"),
        P("tensor"),
        P("tensor"),
        P("tensor"),
        P(None, "tensor"),
        P("tensor"),
        P("tensor", None),
        P("tensor"),
        P("tensor"),
    )
    return jax.shard_map(
        functools.partial(per_device, mesh.shape["tensor"], mesh.shape["dp"]),
        mesh=mesh,
        in_specs=in_specs,
        out_specs=out_specs,
        check_vma=False,
    )
```

time: 3660 us -> 764 us (0.21)
  waiting for transfers between devices: 2520 us -> 243 us
  matrix products: 582 us -> 0 us
  local copies, waits for them, and re-layouts: 344 us -> 42.5 us
  blocking collectives: 0 us -> 218 us
  Pallas kernels: 0 us -> 190 us
  other arithmetic: 179 us -> 19.9 us
    psum x3 -> x0, waiting for transfers between devices: 1250 us -> none  [the longest x1 1210 us: per_device(): grad_normed = lax.psum(grad_normed_part, 'tensor')]
    all_gather x2 -> x3, waiting for transfers between devices: 656 us -> 0.02 us  [the longest x1 0.02 us: per_device(): wout = lax.all_gather(w_out, 'tensor', axis=0, tiled=True)]
    dot_general x16 -> x0, matrix products: 582 us -> none  [the longest x3 218 us: mixer_first(): jnp.einsum('chk,cnakbw->cnahbw', kern_height, masked, precision=lax.Preci...]
    unnamed x7 -> x6, waiting for transfers between devices: 623 us -> 102 us
    pallas_call x0 -> x9, Pallas kernels: none -> 190 us  [the longest x3 59.9 us: mix_bwd(): pl.pallas_call(mix_bwd_kernel, grid=(1,), out_shape=(jax.ShapeDtypeStruct...]
    all_to_all x0 -> x5, waiting for transfers between devices: none -> 141 us  [exchange(): return lax.all_to_all(a, 'tensor', 0, 0, tiled=True)]
    all_gather x0 -> x2, blocking collectives: none -> 135 us  [the longest x1 124 us: per_device(): kern = lax.all_gather(kern, 'tensor')]
    unnamed x123 -> x67, local copies, waits for them, and re-layouts: 105 us -> 8.25 us
  transfers between devices with their start and end apart: 6 -> 10, of which waited for: 5 -> 4; matrix products, arithmetic and copies ran while one was open for 16% -> 7% of each run, Pallas kernels for 0% -> 15%
where the time goes in v1:
time: 764 us; the launch traced here: 760 us
  waiting for transfers between devices  243 us (32%)
  blocking collectives  218 us (29%)
  Pallas kernels  190 us (25%)
  local copies, waits for them, and re-layouts  42.5 us (6%)
  starting transfers between devices  32.2 us (4%)
  other arithmetic  19.9 us (3%)
  between operations  14.3 us (2%)
    all_to_all x5, waiting for transfers between devices, exchange(): return lax.all_to_all(a, 'tensor', 0, 0, tiled=True)  141 us
    all_gather x1, blocking collectives, per_device(): kern = lax.all_gather(kern, 'tensor')  124 us
    unnamed x6, waiting for transfers between devices  102 us
    pallas_call x3, Pallas kernels, mix_bwd(): pl.pallas_call(mix_bwd_kernel, grid=(1,), out_shape=(jax.ShapeDtypeStruct...  59.9 us
    pallas_call x1, Pallas kernels, ff_bwd(): pl.pallas_call(ff_bwd_kernel, grid=(pix // STEP,), out_shape=shapes, in_s...  55.5 us
    all_to_all x1, blocking collectives, exchange(): return lax.all_to_all(a, 'tensor', 0, 0, tiled=True)  41.6 us
    psum x1, blocking collectives, per_device(): lax.psum((vec, jnp.sum(g_bin, axis=1), gk), ('dp', 'tensor'))  41.3 us
    pallas_call x1, Pallas kernels, ff_fwd(): pl.pallas_call(ff_fwd_kernel, grid=(pix // STEP,), out_shape=(jax.ShapeDt...  40.8 us
  transfers between devices with their start and end apart: 10, of which 4 were waited for; matrix products, arithmetic and copies ran while one was open for 7% of the time, Pallas kernels for 15%

profile of v1, /device:TPU:24, one launch (start us, length us, event | category | flops | bytes accessed | tf_op | source)
XLA Modules:
  0.0 759.8 jit_solution(18028501916638703919)
XLA Ops:
  7.2 4.9 copy.111
  12.1 5.1 all-to-all-start
  17.9 122.6 %all-to-all-done = bf16[4,96,6272]{2,1,0:T(8,128)(2,1)} async-done(((bf16[4,96,6272]{2,1,0:T(8,128)(2,1)}), bf16[4,96,6272]{2,1,0:T(8,128)(2,1)}, u32[]{:S(2)}, u32[]{:S(2)}) %all-to-all-start) | async-done | bytes 4816928 | tf_op jit(solution)/shard_map/all_to_all | solution.py:385
  140.5 4.9 copy.110
  145.6 7.5 all-to-all-start.1
  154.5 3.6 multiply_reduce_fusion.5
  158.3 124.1 %all-gather = f32[128,96]{1,0:T(8,128)S(1)} all-gather(f32[32,96]{1,0:T(8,128)S(1)} %maximum_maximum_fusion), channel_id=2, replica_groups=mesh['dp'=8,'tensor'=4] {'tensor'}, dimensions={0}, use_global_device_ids=true | all-gather | bytes 61440 | tf_op jit(solution)/shard_map/all_gather | solution.py:398
  285.3 10.6 %all-gather.2 = f32[4,1,384]{2,1,0:T(1,128)S(1)} all-gather(f32[1,1,384]{2,1,0:T(1,128)S(1)} %reshape.210), channel_id=1, replica_groups=mesh['dp'=8,'tensor'=4] {'tensor'}, dimensions={0}, use_global_device_ids=true | all-gather | bytes 7680 | tf_op jit(solution)/shard_map/all_gather | solution.py:407
  296.0 2.4 copy.96.wout_t
  298.5 2.4 copy.95.win_t
  301.8 27.2 %mix_fwd.1 = bf16[4,3,32,6272]{3,2,1,0:T(8,128)(2,1)} custom-call(bf16[4,3,32,6272]{3,2,1,0:T(8,128)(2,1)} %bitcast.4.x_ref, f32[32,384]{1,0:T(8,128)} %reshape.192.kern_ref, f32[4,28,8,128]{3,2,1,0:T(8,128)} %broadcast_in_dim.12.mask_ref), custom_call_target="tpu_custom_call" | custom-call | flops 24999999488 | bytes 10000000 | tf_op jit(solution)/shard_map/mix_fwd/pallas_call | solution.py:97
  330.2 40.8 %ff_fwd.1 = (bf16[384,6272]{1,0:T(8,128)(2,1)}, bf16[1536,6272]{1,0:T(8,128)(2,1)}, bf16[1536,6272]{1,0:T(8,128)(2,1)}) custom-call(bf16[384,6272]{1,0:T(8,128)(2,1)} %bitcast.101, bf16[384,6272]{1,0:T(8,128)(2,1)} %bitcast.14.x_ref, bf16[1536,384]{1,0:T(8,128)(2,1)} %copy.95.win_t, bf16[384,1536]{1,0:T(8,128)(2,1)} %copy.96.wout_t, ...), custom_call_target="tpu_custom_call" | custom-call | flops 14797504512 | bytes 60000000 | tf_op jit(solution)/shard_map/ff_fwd/pallas_call | solution.py:237
  371.0 55.5 %ff_bwd.1 = (f32[384,6272]{1,0:T(8,128)}, f32[1536,384]{1,0:T(8,128)}, f32[1536,384]{1,0:T(8,128)}, f32[1536,128]{1,0:T(8,128)}, f32[4,384,128]{2,1,0:T(8,128)}) custom-call(bf16[384,6272]{1,0:T(8,128)(2,1)} %bitcast.19.go_ref, bf16[384,6272]{1,0:T(8,128)(2,1)} %bitcast.102, bf16[1536,6272]{1,0:T(8,128)(2,1)} %get-tuple-element.50.hid_ref, ...), custom_call_target="tpu_custom_call" | custom-call | flops 29595009024 | bytes 70000000 | tf_op jit(solution)/shard_map/ff_bwd/pallas_call | solution.py:302
  426.5 20.0 %mix_bwd.3 = (bf16[4,32,6272]{2,1,0:T(8,128)(2,1)}, f32[32,128]{1,0:T(8,128)}) custom-call(bf16[4,3,32,6272]{3,2,1,0:T(8,128)(2,1)} %bitcast.4.x_ref, f32[4,3,32,6272]{3,2,1,0:T(8,128)} %bitcast.98, f32[32,384]{1,0:T(8,128)} %reshape.192.kern_ref, f32[4,28,8,128]{3,2,1,0:T(8,128)} %broadcast_in_dim.12.mask_ref), custom_call_target="tpu_custom_call" | custom-call | flops 20000000000 | bytes 10000000 | tf_op jit(solution)/shard_map/mix_bwd/pallas_call | solution.py:179
  446.5 6.1 all-to-all-start.3
  452.6 20.0 %mix_bwd.4 = (bf16[4,32,6272]{2,1,0:T(8,128)(2,1)}, f32[32,128]{1,0:T(8,128)}) custom-call(bf16[4,3,32,6272]{3,2,1,0:T(8,128)(2,1)} %bitcast.4.x_ref, f32[4,3,32,6272]{3,2,1,0:T(8,128)} %bitcast.99, f32[32,384]{1,0:T(8,128)} %reshape.192.kern_ref, f32[4,28,8,128]{3,2,1,0:T(8,128)} %broadcast_in_dim.12.mask_ref), custom_call_target="tpu_custom_call" | custom-call | flops 20000000000 | bytes 10000000 | tf_op jit(solution)/shard_map/mix_bwd/pallas_call | solution.py:179
  472.6 10.2 %all-to-all-done.3.g_ref = bf16[4,32,6272]{2,1,0:T(8,128)(2,1)S(1)} async-done(((bf16[4,32,6272]{2,1,0:T(8,128)(2,1)}), bf16[4,32,6272]{2,1,0:T(8,128)(2,1)S(1)}, u32[]{:S(2)}, u32[]{:S(2)}) %all-to-all-start.3) | async-done | bytes 1605664 | tf_op jit(solution)/shard_map/all_to_all | solution.py:385
  482.9 5.9 all-to-all-start.4
  488.8 2.7 pad_maximum_fusion
  491.5 2.7 copy.104
  494.3 20.0 %mix_bwd.5 = (bf16[4,32,6272]{2,1,0:T(8,128)(2,1)}, f32[32,128]{1,0:T(8,128)}) custom-call(bf16[4,3,32,6272]{3,2,1,0:T(8,128)(2,1)} %bitcast.4.x_ref, f32[4,3,32,6272]{3,2,1,0:T(8,128)} %bitcast.100, f32[32,384]{1,0:T(8,128)} %reshape.192.kern_ref, f32[4,28,8,128]{3,2,1,0:T(8,128)} %broadcast_in_dim.12.mask_ref), custom_call_target="tpu_custom_call" | custom-call | flops 20000000000 | bytes 10000000 | tf_op jit(solution)/shard_map/mix_bwd/pallas_call | solution.py:179
  514.2 8.2 %all-to-all-done.4.g_ref = bf16[4,32,6272]{2,1,0:T(8,128)(2,1)S(1)} async-done(((bf16[4,32,6272]{2,1,0:T(8,128)(2,1)}), bf16[4,32,6272]{2,1,0:T(8,128)(2,1)S(1)}, u32[]{:S(2)}, u32[]{:S(2)}) %all-to-all-start.4) | async-done | bytes 1605664 | tf_op jit(solution)/shard_map/all_to_all | solution.py:385
  522.4 41.6 %all_to_all.30.g_ref = bf16[4,32,6272]{2,1,0:T(8,128)(2,1)} all-to-all(bf16[4,32,6272]{2,1,0:T(8,128)(2,1)} %get-tuple-element.55), channel_id=1, replica_groups=mesh['dp'=8,'tensor'=4] {'tensor'}, dimensions={0} | all-to-all | bytes 3211264 | tf_op jit(solution)/shard_map/all_to_all | solution.py:385
  564.0 7.5 all-to-all-start.2
  572.8 99.9 %all-reduce.7.cloned.1.call-done = f32[2,4,48,384]{3,2,1,0:T(8,128)} async-done(((f32[2,4,48,384]{3,2,1,0:T(8,128)}), f32[2,4,48,384]{3,2,1,0:T(8,128)}) %all-reduce.7.cloned.1.call-update) | async-done | bytes 589840
  674.9 2.3 multiply_reduce_fusion
  680.9 41.3 %all-reduce.4 = (f32[3,32,128]{2,1,0:T(8,128)}, f32[4,384]{1,0:T(4,128)}, f32[1536]{0:T(1024)}) all-reduce(f32[3,32,128]{2,1,0:T(8,128)S(1)} %pad_maximum_fusion.2, f32[4,384]{1,0:T(4,128)S(1)} %scatter.4, f32[1536]{0:T(1024)S(1)} %reduce_sum.139), channel_id=1, replica_groups=mesh['dp'=8,'tensor'=4] {'dp','tensor'}, use_global_device_ids=true, to_apply=%region_1.2 | all-reduce | flops 15360 | bytes 122880 | tf_op jit(solution)/shard_map/psum | solution.py:444
  726.5 5.0 multiply_reduce_fusion.1
  734.5 2.4 copy-done
  738.3 2.3 finish.3.rest_0_
  740.6 2.3 finish.4.rest_0_
  745.2 4.9 copy.107
  (136 shorter events, 28.5 us)
Async XLA Ops:
  12.1 128.4 %all-to-all-start = ((bf16[4,96,6272]{2,1,0:T(8,128)(2,1)}), bf16[4,96,6272]{2,1,0:T(8,128)(2,1)}, u32[]{:S(2)}, u32[]{:S(2)}) async-start(bf16[4,96,6272]{2,1,0:T(8,128)(2,1)} %bitcast.78), calls=%async_computation | async-start | bytes 9633792 | tf_op jit(solution)/shard_map/all_to_all | solution.py:385
  17.2 278.8 %all-gather.9.cloned.1.call-start = ((), (), s32[]{:S(2)}) async-start(), calls=%async_computation.8 | async-start | bytes 1474560 | tf_op jit(solution)/shard_map/all_gather | solution.py:406
  145.4 8.5 %copy-start.13 = (f32[2,96,64]{1,2,0:T(8,128)S(1)}, f32[2,96,64]{1,2,0:T(8,128)}, u32[]{:S(2)}) copy-start(f32[2,96,64]{1,2,0:T(8,128)} %param.25) | copy-start | bytes 147460
  145.4 8.5 %copy-start.6 = (f32[96,64]{0,1:T(8,128)S(1)}, f32[96,64]{0,1:T(8,128)}, u32[]{:S(2)}) copy-start(f32[96,64]{0,1:T(8,128)} %param.23) | copy-start | bytes 73732
  145.5 12.7 %copy-start.29 = (f32[96]{0:T(128)S(1)}, f32[96]{0:T(128)}, u32[]{:S(2)}) copy-start(f32[96]{0:T(128)} %param.27) | copy-start | bytes 1156
  145.5 138.0 %copy-start.24 = (s32[32,4,2]{0,2,1:T(2,128)S(1)}, s32[32,4,2]{0,2,1:T(2,128)}, u32[]{:S(2)}) copy-start(s32[32,4,2]{0,2,1:T(2,128)} %param.21) | copy-start | bytes 3076
  145.5 138.0 %copy-start.25 = (s32[32,4,2]{0,2,1:T(2,128)S(1)}, s32[32,4,2]{0,2,1:T(2,128)}, u32[]{:S(2)}) copy-start(s32[32,4,2]{0,2,1:T(2,128)} %param.20) | copy-start | bytes 3076
  145.5 138.9 %copy-start.20 = (f32[384]{0:T(512)S(1)}, f32[384]{0:T(512)}, u32[]{:S(2)}) copy-start(f32[384]{0:T(512)} %param.34) | copy-start | bytes 4612
  145.5 138.9 %copy-start.21 = (f32[384]{0:T(512)S(1)}, f32[384]{0:T(512)}, u32[]{:S(2)}) copy-start(f32[384]{0:T(512)} %param.33) | copy-start | bytes 4612
  145.5 138.9 %copy-start.26 = (f32[384]{0:T(512)S(1)}, f32[384]{0:T(512)}, u32[]{:S(2)}) copy-start(f32[384]{0:T(512)} %param.29) | copy-start | bytes 4612
  145.5 138.9 %copy-start.27 = (f32[384]{0:T(512)S(1)}, f32[384]{0:T(512)}, u32[]{:S(2)}) copy-start(f32[384]{0:T(512)} %param.28) | copy-start | bytes 4612
  145.5 139.8 %copy-start.28 = (f32[384]{0:T(512)S(1)}, f32[384]{0:T(512)}, u32[]{:S(2)}) copy-start(f32[384]{0:T(512)} %param.31) | copy-start | bytes 4612
  145.6 225.4 %all-to-all-start.1 = ((bf16[4,96,6272]{2,1,0:T(8,128)(2,1)}), bf16[4,96,6272]{2,1,0:T(8,128)(2,1)}, u32[]{:S(2)}, u32[]{:S(2)}) async-start(bf16[4,96,6272]{2,1,0:T(8,128)(2,1)} %bitcast.77), calls=%async_computation.1 | async-start | bytes 9633792 | tf_op jit(solution)/shard_map/all_to_all | solution.py:385
  153.1 145.4 %all-gather.7.cloned.1.call-start = ((), (), s32[]{:S(2)}) async-start(), calls=%async_computation.7 | async-start | bytes 1474560 | tf_op jit(solution)/shard_map/all_gather | solution.py:405
  153.9 128.5 %copy-start.2 = (f32[96,64]{0,1:T(8,128)}, f32[96,64]{0,1:T(8,128)S(1)}, u32[]{:S(2)}) copy-start(f32[96,64]{0,1:T(8,128)S(1)} %exp.10) | copy-start | bytes 73732
  154.0 128.6 %copy-start.15 = (f32[2,96,64]{1,2,0:T(8,128)}, f32[2,96,64]{1,2,0:T(8,128)S(1)}, u32[]{:S(2)}) copy-start(f32[2,96,64]{1,2,0:T(8,128)S(1)} %get-tuple-element.141) | copy-start | bytes 147460
  154.0 128.3 %copy-start.8 = (f32[2,96,64]{1,2,0:T(8,128)}, f32[2,96,64]{1,2,0:T(8,128)S(1)}, u32[]{:S(2)}) copy-start(f32[2,96,64]{1,2,0:T(8,128)S(1)} %get-tuple-element.150) | copy-start | bytes 147460
  446.5 36.4 %all-to-all-start.3 = ((bf16[4,32,6272]{2,1,0:T(8,128)(2,1)}), bf16[4,32,6272]{2,1,0:T(8,128)(2,1)S(1)}, u32[]{:S(2)}, u32[]{:S(2)}) async-start(bf16[4,32,6272]{2,1,0:T(8,128)(2,1)} %get-tuple-element.53), calls=%async_computation.3 | async-start | bytes 3211264 | tf_op jit(solution)/shard_map/all_to_all | solution.py:385
  482.9 39.5 %all-to-all-start.4 = ((bf16[4,32,6272]{2,1,0:T(8,128)(2,1)}), bf16[4,32,6272]{2,1,0:T(8,128)(2,1)S(1)}, u32[]{:S(2)}, u32[]{:S(2)}) async-start(bf16[4,32,6272]{2,1,0:T(8,128)(2,1)} %get-tuple-element.54), calls=%async_computation.4 | async-start | bytes 3211264 | tf_op jit(solution)/shard_map/all_to_all | solution.py:385
  488.8 82.8 %reduce-scatter.3.cloned.1.call-start = ((), (), s32[]{:S(2)}) async-start(), calls=%async_computation.9 | async-start | bytes 5308416 | tf_op jit(solution)/shard_map/reduce_scatter | solution.py:436
  564.0 181.2 %all-to-all-start.2 = ((bf16[4,96,6272]{2,1,0:T(8,128)(2,1)}), bf16[4,96,6272]{2,1,0:T(8,128)(2,1)}, u32[]{:S(2)}, u32[]{:S(2)}) async-start(bf16[4,96,6272]{2,1,0:T(8,128)(2,1)} %bitcast.81), calls=%async_computation.2 | async-start | bytes 9633792 | tf_op jit(solution)/shard_map/all_to_all | solution.py:385
  571.5 108.7 %copy-start.16 = (f32[32,128]{1,0:T(8,128)S(1)}, f32[32,128]{1,0:T(8,128)}, u32[]{:S(2)}) copy-start(f32[32,128]{1,0:T(8,128)} %get-tuple-element.58) | copy-start | bytes 49156
  571.5 108.7 %copy-start.17 = (f32[32,128]{1,0:T(8,128)S(1)}, f32[32,128]{1,0:T(8,128)}, u32[]{:S(2)}) copy-start(f32[32,128]{1,0:T(8,128)} %get-tuple-element.57) | copy-start | bytes 49156
  571.5 155.0 %copy-start.9 = (f32[2,96,64]{1,2,0:T(8,128)S(1)}, f32[2,96,64]{1,2,0:T(8,128)}, u32[]{:S(2)}) copy-start(f32[2,96,64]{1,2,0:T(8,128)} %copy-done.8) | copy-start | bytes 147460
  571.5 155.0 %copy-start.11 = (f32[2,96,64]{1,2,0:T(8,128)S(1)}, f32[2,96,64]{1,2,0:T(8,128)}, u32[]{:S(2)}) copy-start(f32[2,96,64]{1,2,0:T(8,128)} %copy-done.10) | copy-start | bytes 147460
  571.5 160.7 %copy-start.3 = (f32[96,64]{0,1:T(8,128)S(1)}, f32[96,64]{0,1:T(8,128)}, u32[]{:S(2)}) copy-start(f32[96,64]{0,1:T(8,128)} %copy-done.2) | copy-start | bytes 73732
  571.5 160.7 %copy-start.7 = (f32[96,64]{0,1:T(8,128)S(1)}, f32[96,64]{0,1:T(8,128)}, u32[]{:S(2)}) copy-start(f32[96,64]{0,1:T(8,128)} %param.23) | copy-start | bytes 73732
  571.5 160.7 %copy-start.19 = (f32[2,96]{1,0:T(2,128)S(1)}, f32[2,96]{1,0:T(2,128)}, u32[]{:S(2)}) copy-start(f32[2,96]{1,0:T(2,128)} %copy-done.18) | copy-start | bytes 2308
  571.5 161.8 %copy-start.23 = (f32[2,96]{1,0:T(2,128)S(1)}, f32[2,96]{1,0:T(2,128)}, u32[]{:S(2)}) copy-start(f32[2,96]{1,0:T(2,128)} %param.26) | copy-start | bytes 2308
  571.5 162.4 %copy-start.5 = (f32[96,64]{0,1:T(8,128)S(1)}, f32[96,64]{0,1:T(8,128)}, u32[]{:S(2)}) copy-start(f32[96,64]{0,1:T(8,128)} %param.22) | copy-start | bytes 73732
  571.5 101.1 %all-reduce.7.cloned.1.call-start = ((), (), s32[]{:S(2)}) async-start(), calls=%async_computation.11 | async-start | bytes 1179648
  572.1 178.0 %all-gather.11.cloned.1.call-start = ((), (), s32[]{:S(2)}) async-start(), calls=%async_computation.10 | async-start | bytes 1327104 | tf_op jit(solution)/shard_map/all_gather | solution.py:438
  (9 other events, 46.3 us)
Sparse Core Ops, SparseCore 0:
  19.6 55.4 all-gather.8
  155.5 94.9 all-gather.6
  494.4 54.9 reduce-scatter.2
  574.5 98.0 all-reduce.6
  675.2 25.3 all-gather.10

commit v2 on v0

v2 whole, which is shorter than its diff:
```python
import functools

import jax
import jax.numpy as jnp
from jax import lax
from jax.experimental import pallas as pl
from jax.experimental.pallas import tpu as pltpu
from jax.sharding import PartitionSpec as P

F32, BF16 = jnp.float32, jnp.bfloat16
CROP = 14
SIDE = 2 * CROP
NPIX = SIDE * SIDE
LANES = 128
GROUP = 32
STEP = 896
EPS = 1e-06
GELU_C = 0.7978845608028654
GELU_A = 0.044715
VMEM = 63 << 20
MESH = pl.DeviceIdType.MESH


def nn(a, b):
    return lax.dot_general(a, b, (((1,), (0,)), ((), ())), preferred_element_type=F32)


def nt(a, b):
    return lax.dot_general(a, b, (((1,), (1,)), ((), ())), preferred_element_type=F32)


def conv(y, taps):
    return [sum((taps[l] * y[i - l] for l in range(1, i + 1)), taps[0] * y[i]) for i in range(CROP)]


def conv_back(y, taps):
    return [
        sum((taps[l] * y[i + l] for l in range(1, CROP - i)), taps[0] * y[i]) for i in range(CROP)
    ]


def spot(slot, h, w):
    first = (slot // 2) * (CROP * SIDE) + (slot % 2) * CROP
    return pl.ds(first + h * SIDE + w, 8, stride=NPIX)


def lanes_to_rows(load, rows):
    @pl.loop(0, rows.shape[0] // STEP)
    def _(j):
        off = pl.multiple_of(j * STEP, LANES)
        rows[pl.ds(off, STEP), :] = jnp.transpose(load(off).astype(F32))


def rows_to_lanes(rows, store):
    @pl.loop(0, rows.shape[0] // STEP)
    def _(j):
        off = pl.multiple_of(j * STEP, LANES)
        store(off, jnp.transpose(rows[pl.ds(off, STEP), :]).astype(BF16))


def tap_rows(kern, q, base):
    return [jnp.broadcast_to(kern[q, pl.ds(base + l, 1), :], (8, LANES)) for l in range(CROP)]


def tile_of(ref, q, off):
    return ref[:, pl.ds(pl.multiple_of(q * GROUP, GROUP), GROUP), pl.ds(off, STEP)].reshape(
        LANES, STEP
    )


def put_tile(ref, q, off, v):
    ref[:, pl.ds(pl.multiple_of(q * GROUP, GROUP), GROUP), pl.ds(off, STEP)] = v.reshape(
        ref.shape[0], GROUP, STEP
    )


def along_width(q, slot, rows, kern, mask, inner):
    @pl.loop(0, CROP)
    def _(h):
        taps = tap_rows(kern, q, CROP)
        row_in = mask[slot, h]
        y = [rows[spot(slot, h, w), :] * mask[slot, CROP + w] for w in range(CROP)]
        for w, v in enumerate(conv(y, taps)):
            inner[h, w] = v * row_in


def mix_fwd(q, x_all, rows, kern, mask, inner, mixed):
    lanes_to_rows(lambda off: tile_of(x_all, q, off), rows)
    skip = jnp.broadcast_to(kern[q, pl.ds(2 * CROP, 1), :], (8, LANES))

    @pl.loop(0, 4)
    def _(slot):
        along_width(q, slot, rows, kern, mask, inner)

        @pl.loop(0, CROP)
        def _(w):
            taps = tap_rows(kern, q, 0)
            col_in = mask[slot, CROP + w]
            y = [inner[h, w] for h in range(CROP)]
            for h, v in enumerate(conv(y, taps)):
                at = spot(slot, h, w)
                rows[at, :] = v * (mask[slot, h] * col_in) + skip * rows[at, :]

    rows_to_lanes(rows, lambda off, v: put_tile(mixed, q, off, v))


def mix_bwd(q, x_all, rows, grow, kern, mask, inner, mid, out, gkern):
    lanes_to_rows(lambda off: tile_of(x_all, q, off), rows)
    skip = jnp.broadcast_to(kern[q, pl.ds(2 * CROP, 1), :], (8, LANES))
    zero = jnp.zeros((8, LANES), F32)

    def per_slot(slot, sums):
        gk_height, gk_width, gskip = sums
        along_width(q, slot, rows, kern, mask, inner)

        def down(w, acc):
            taps = tap_rows(kern, q, 0)
            col_in = mask[slot, CROP + w]
            u = [grow[q, spot(slot, h, w), :] * (mask[slot, h] * col_in) for h in range(CROP)]
            for h, v in enumerate(conv_back(u, taps)):
                mid[h, w] = v * mask[slot, h]
            a = [inner[h, w] for h in range(CROP)]
            return tuple(
                sum((u[h] * a[h - l] for h in range(l, CROP)), acc[l]) for l in range(CROP)
            )

        gk_height = lax.fori_loop(0, CROP, down, gk_height)

        def across(h, acc):
            gk_width, gskip = acc
            taps = tap_rows(kern, q, CROP)
            u = [mid[h, w] for w in range(CROP)]
            x = [rows[spot(slot, h, w), :] for w in range(CROP)]
            y = [x[w] * mask[slot, CROP + w] for w in range(CROP)]
            gk_width = tuple(
                sum((u[w] * y[w - l] for w in range(l, CROP)), gk_width[l]) for l in range(CROP)
            )
            for w, v in enumerate(conv_back(u, taps)):
                at = spot(slot, h, w)
                g = grow[q, at, :]
                gskip = gskip + g * x[w]
                grow[q, at, :] = v * mask[slot, CROP + w] + skip * g
            return gk_width, gskip

        gk_width, gskip = lax.fori_loop(0, CROP, across, (gk_width, gskip))
        return gk_height, gk_width, gskip

    gk_height, gk_width, gskip = lax.fori_loop(
        0, 4, per_slot, ((zero,) * CROP, (zero,) * CROP, zero)
    )
    gkern[q] = jnp.zeros((LANES, LANES), F32)
    for row, v in enumerate((*gk_height, *gk_width, gskip)):
        gkern[q, pl.ds(row, 1), :] = jnp.sum(v, axis=0, keepdims=True)
    rows_to_lanes(grow.at[q], lambda off, v: put_tile(out, q, off, v))


def lag_waves(step, a_log, a_imag):
    rate = -step * jnp.exp(a_log)
    phase = step * a_imag
    size = jnp.exp(rate)
    re1, im1 = size * jnp.cos(phase), size * jnp.sin(phase)
    re, im = jnp.ones_like(re1), jnp.zeros_like(im1)
    out = []
    for _ in range(CROP):
        out.append((re, im))
        re, im = re * re1 - im * im1, re * im1 + im * re1
    return rate, phase, out


def column_set(acc, k, col):
    lane = lax.broadcasted_iota(jnp.int32, acc.shape, 1)
    return jnp.where(lane == k, col, acc)


def lag_kernels(steps, skip, a_log, a_imag, coefs):
    acc = jnp.zeros((a_log.shape[0], LANES), F32)
    for j in range(2):
        _, _, waves = lag_waves(steps[j], a_log[...], a_imag[...])
        for l, (re, im) in enumerate(waves):
            col = jnp.sum(coefs[j][0] * re - coefs[j][1] * im, axis=1, keepdims=True)
            acc = column_set(acc, CROP * j + l, col)
    return column_set(acc, 2 * CROP, skip)


def lag_grads(cols, steps, a_log, a_imag, coefs, g_alog, g_aimag, g_coefs):
    ga, gi, gdt = 0.0, 0.0, []
    for j in range(2):
        rate, phase, waves = lag_waves(steps[j], a_log[...], a_imag[...])
        cre, cim = coefs[j][0], coefs[j][1]
        g_re = g_im = p = r = 0.0
        for l, (re, im) in enumerate(waves):
            g = cols[:, CROP * j + l : CROP * j + l + 1]
            g_re = g_re + g * re
            g_im = g_im - g * im
            if l:
                p = p + (l * g) * (cre * re - cim * im)
                r = r - (l * g) * (cre * im + cim * re)
        g_coefs[j][0] = g_re
        g_coefs[j][1] = g_im
        ga = ga + p * rate
        gi = gi + r * steps[j]
        gdt.append(jnp.sum(p * rate + r * phase, axis=1, keepdims=True))
    g_alog[...] = ga
    g_aimag[...] = gi
    return gdt


def norm(m):
    centered = m - jnp.mean(m, axis=0, keepdims=True)
    scale = lax.rsqrt(jnp.mean(centered * centered, axis=0, keepdims=True) + EPS)
    return centered * scale, scale


def fold(v):
    return sum(
        (v[:, i * LANES : (i + 1) * LANES] for i in range(1, v.shape[1] // LANES)), v[:, :LANES]
    )


def block_kernel(
    parts,
    groups,
    x,
    go,
    size_ref,
    offset_ref,
    a_log,
    a_imag,
    c_height,
    c_width,
    log_dt,
    skip_gain,
    ln_gain,
    ln_bias,
    w_in,
    b_in,
    w_out,
    b_out,
    layer_scale,
    res_own,
    g_own,
    dw_own,
    g_alog,
    g_aimag,
    g_height,
    g_width,
    row_own,
    go_all,
    hid_far,
    slope_far,
    res,
    dw_peer,
    x_all,
    mixed,
    res_near,
    rows,
    grow,
    inner,
    mid,
    mask,
    kern_mine,
    kern_all,
    kern,
    gkern,
    bin_mine,
    bin_all,
    bin_col,
    chan,
    square,
    win,
    win_t,
    wout,
    wout_t,
    hid,
    slope,
    gp,
    go_near,
    dw,
    dw_sum,
    dw_tensor,
    dw_done,
    bin_acc,
    vec,
    col_mine,
    col_peer,
    col_sum,
    col_tensor,
    send,
    recv,
    own,
    hid_sem,
    slope_sem,
    go_sem,
    res_sem,
    gx_send,
    gx_recv,
    gx_own,
):
    local, pix = x_all.shape[1], x_all.shape[2]
    width = local * parts
    ff = win_t.shape[0]
    shard = ff // parts
    slab = shard // groups
    chunks = pix // STEP
    me = lax.axis_index("tensor")
    dp = lax.axis_index("dp")
    mine = lax.rem(dp, groups)
    first = dp - mine
    across = [{"tensor": lax.rem(me + s, parts)} for s in range(1, parts)]
    beside = [{"dp": first + lax.rem(mine + s, groups)} for s in range(1, groups)]

    barrier = pltpu.get_barrier_semaphore()
    for peer in across + beside:
        pl.semaphore_signal(barrier, inc=1, device_id=peer, device_id_type=MESH)
    pl.semaphore_wait(barrier, len(across) + len(beside))

    count = [0, 0]

    def remote(src, dst, peer, sems=None):
        if sems is None:
            sems = (send.at[count[0]], recv.at[count[0]])
            count[0] += 1
        copy = pltpu.make_async_remote_copy(
            src_ref=src,
            dst_ref=dst,
            send_sem=sems[0],
            recv_sem=sems[1],
            device_id=peer,
            device_id_type=MESH,
        )
        copy.start()
        return copy

    def near(src, dst, sem=None):
        if sem is None:
            sem = own.at[count[1]]
            count[1] += 1
        copy = pltpu.make_async_copy(src, dst, sem)
        copy.start()
        return copy

    sent = []

    def arrived(copies):
        for copy in copies:
            copy.wait_recv()
        sent.extend(copies)

    def pixels(ref, peer):
        return ref.at[:, pl.ds(pl.multiple_of(peer * pix, LANES), pix)]

    def to_owner(ref, out):
        copies = [remote(pixels(ref, p["tensor"]), out.at[me], p) for p in across]
        return copies, near(pixels(ref, me), out.at[me])

    x_copies, x_near = to_owner(x, x_all)
    my_slab = pl.ds(pl.multiple_of(mine * slab, slab), slab)
    my_cols = pl.ds(pl.multiple_of(me * shard, LANES), shard)
    w_near = [
        near(w_in.at[my_slab, :], win.at[my_slab, my_cols]),
        near(w_out.at[my_slab, :], wout.at[me, my_slab, :]),
    ]
    w_copies = [remote(w_in.at[my_slab, :], win.at[my_slab, my_cols], p) for p in across]
    w_copies += [remote(w_out.at[my_slab, :], wout.at[me, my_slab, :], p) for p in across]

    square[...] = jnp.zeros_like(square)
    square[0:2, 0:local] = log_dt[...]
    square[2:3, 0:local] = skip_gain[...]
    turned = jnp.transpose(square[:, 0:LANES])
    steps = [jnp.exp(turned[0:local, j : j + 1]) for j in range(2)]
    coefs = [c_height, c_width]
    kern_mine[...] = lag_kernels(steps, turned[0:local, 2:3], a_log, a_imag, coefs)
    bin_mine[...] = jnp.broadcast_to(b_in[...], bin_mine.shape)
    kern_all[me] = kern_mine[...]
    bin_all[me] = bin_mine[...]
    k_copies = [remote(kern_mine, kern_all.at[me], p) for p in across]
    k_copies += [remote(bin_mine, bin_all.at[me], p) for p in across]

    for copy in w_near:
        copy.wait()
    arrived(w_copies)
    w_copies = [remote(win.at[my_slab, :], win.at[my_slab, :], p) for p in beside]
    w_copies += [remote(wout.at[:, my_slab, :], wout.at[:, my_slab, :], p) for p in beside]

    row = 0
    for ref in (ln_gain, ln_bias, b_out, layer_scale):
        square[row : row + 1, :] = ref[...]
        row += 1
    for i in range(width // LANES):
        chan[i * LANES : (i + 1) * LANES, :] = jnp.transpose(square[:, i * LANES : (i + 1) * LANES])
    at = pl.ds(pl.multiple_of(me * 8, 8), 8)
    lo, extent = offset_ref[at, :], size_ref[at, :]
    for slot in range(4):
        for j in range(2):
            k = 2 * slot + j
            low = jnp.broadcast_to(lo[:, k : k + 1], (8, LANES))
            high = low + jnp.broadcast_to(extent[:, k : k + 1], (8, LANES))
            for s in range(CROP):
                mask[slot, CROP * j + s] = jnp.where((low <= s) & (s < high), 1.0, 0.0)
    arrived(k_copies)
    for q in range(local // GROUP):
        part = kern_all[:, q * GROUP : (q + 1) * GROUP, :].reshape(LANES, LANES)
        kern[q] = jnp.transpose(part)
    for t in range(parts):
        for i in range(shard // LANES):
            block = jnp.broadcast_to(bin_all[t, 0:1, i * LANES : (i + 1) * LANES], (LANES, LANES))
            bin_col[t * shard + i * LANES : t * shard + (i + 1) * LANES, :] = jnp.transpose(block)
    arrived(w_copies)
    for t in range(parts):
        cols = slice(t * shard, (t + 1) * shard)
        win_t[cols, :] = jnp.transpose(win[:, cols].astype(F32)).astype(BF16)
        wout_t[:, cols] = jnp.transpose(wout[t].astype(F32)).astype(BF16)

    arrived(x_copies)
    x_near.wait()
    go_copies, go_own = to_owner(go, go_all)

    @pl.loop(0, local // GROUP)
    def _(q):
        mix_fwd(q, x_all, rows, kern, mask, inner, mixed)

    def hid_copy(t, j, back):
        sl = pl.ds(t * shard, shard)
        lanes = pl.ds(pl.multiple_of(j * STEP, LANES), STEP)
        pair = [(hid.at[sl, :], hid_far.at[sl, lanes]), (slope.at[sl, :], slope_far.at[sl, lanes])]
        pair = [p[::-1] if back else p for p in pair]
        return [
            pltpu.make_async_copy(*p, sem.at[t]) for p, sem in zip(pair, (hid_sem, slope_sem))
        ]

    def res_copy(j):
        lanes = pl.ds(pl.multiple_of(j * STEP, LANES), STEP)
        return pltpu.make_async_copy(res_near, res.at[:, :, lanes], res_sem)

    def low_of(off):
        normed, scale = norm(mixed[:, :, pl.ds(off, STEP)].reshape(width, STEP).astype(F32))
        return normed, scale, (normed * chan[:, 0:1] + chan[:, 1:2]).astype(BF16)

    @pl.loop(0, chunks)
    def _(j):
        off = pl.multiple_of(j * STEP, LANES)
        _, _, low = low_of(off)
        for t in range(parts):
            sl = pl.ds(t * shard, shard)
            pre = nn(win_t[sl, :], low) + bin_col[sl, 0:1]
            square_pre = pre * pre
            th = jnp.tanh(pre * (GELU_C + (GELU_C * GELU_A) * square_pre))
            half = 0.5 * th + 0.5
            inner_slope = GELU_C + (3 * GELU_C * GELU_A) * square_pre

            @pl.when(j > 0)
            def _():
                for copy in hid_copy(t, j, False):
                    copy.wait()

            hid[sl, :] = (pre * half).astype(BF16)
            slope[sl, :] = (half + pre * (0.5 - 0.5 * th * th) * inner_slope).astype(BF16)
            for copy in hid_copy(t, j, False):
                copy.start()
        branch = nn(wout_t[...], hid[...]) + chan[:, 2:3]
        source = x_all[:, :, pl.ds(off, STEP)].reshape(width, STEP).astype(F32)
        out = (source + chan[:, 3:4] * branch).astype(BF16)

        @pl.when(j > 0)
        def _():
            res_copy(j).wait()

        res_near[...] = out.reshape(parts, local, STEP)
        res_copy(j).start()

    for t in range(parts):
        for copy in hid_copy(t, 0, False):
            copy.wait()
        for copy in hid_copy(t, 0, True):
            copy.start()

    res_copy(0).wait()

    arrived(go_copies)
    go_own.wait()
    res_copies = [remote(res.at[p["tensor"]], res_own.at[me], p) for p in across]
    res_mine = near(res.at[me], res_own.at[me])

    for ref in (dw, bin_acc, vec):
        ref[...] = jnp.zeros_like(ref)

    def go_copy(j):
        lanes = pl.ds(pl.multiple_of(j * STEP, LANES), STEP)
        return pltpu.make_async_copy(go_all.at[:, :, lanes], go_near, go_sem)

    go_copy(0).start()

    @pl.loop(0, chunks)
    def _(j):
        off = pl.multiple_of(j * STEP, LANES)
        go_copy(j).wait()
        grad = go_near[...].reshape(width, STEP).astype(F32)
        gb = (grad * chan[:, 3:4]).astype(BF16)
        vec[0] += fold(gb.astype(F32))
        vec[3] += fold(grad)

        @pl.when(j + 1 < chunks)
        def _():
            go_copy(j + 1).start()

        normed, scale, low = low_of(off)
        for t in range(parts):
            sl = pl.ds(t * shard, shard)
            for copy in hid_copy(t, j, True):
                copy.wait()
            tile = (nn(wout[t], gb) * slope[sl, :].astype(F32)).astype(BF16)
            gp[sl, :] = tile
            bin_acc[sl, :] += fold(tile.astype(F32))
            dw[0, t] += nt(hid[sl, :], gb)
            dw[1, t] += nt(tile, low)

            @pl.when(j + 1 < chunks)
            def _():
                for copy in hid_copy(t, j + 1, True):
                    copy.start()

        gn = nn(win[...], gp[...])
        vec[1] += fold(gn * normed)
        vec[2] += fold(gn)
        g1 = gn * chan[:, 0:1]
        m1 = jnp.mean(g1, axis=0, keepdims=True)
        m2 = jnp.mean(g1 * normed, axis=0, keepdims=True)
        gm = (scale * (g1 - m1 - normed * m2)).reshape(parts, local, STEP)
        for q in range(local // GROUP):
            block = gm[:, q * GROUP : (q + 1) * GROUP, :].reshape(LANES, STEP)
            grow[q, pl.ds(off, STEP), :] = jnp.transpose(block)

    def slab_of(peer):
        return pl.ds(pl.multiple_of((peer["dp"] - first) * slab, slab), slab)

    dw_near = near(dw.at[:, :, my_slab, :], dw_peer.at[:, :, my_slab, :])
    dw_copies = [
        remote(dw.at[:, :, slab_of(p), :], dw_peer.at[:, :, my_slab, :], p) for p in beside
    ]

    def gx_tile(q):
        return pl.ds(pl.multiple_of(q * GROUP, GROUP), GROUP)

    def gx_copies(q):
        at = gx_tile(q)
        return [
            pltpu.make_async_remote_copy(
                src_ref=mixed.at[p["tensor"], at, :],
                dst_ref=g_own.at[me, at, :],
                send_sem=gx_send.at[q, s],
                recv_sem=gx_recv.at[q, s],
                device_id=p,
                device_id_type=MESH,
            )
            for s, p in enumerate(across)
        ] + [pltpu.make_async_copy(mixed.at[me, at, :], g_own.at[me, at, :], gx_own.at[q])]

    @pl.loop(0, local // GROUP)
    def _(q):
        mix_bwd(q, x_all, rows, grow, kern, mask, inner, mid, mixed, gkern)
        for copy in gx_copies(q):
            copy.start()

    for q in range(local // GROUP):
        col_mine[:, q * GROUP : (q + 1) * GROUP, :] = jnp.transpose(gkern[q]).reshape(
            parts, GROUP, LANES
        )
    acc = col_mine[...].reshape(width, LANES)
    sums = [jnp.sum(vec[k], axis=1, keepdims=True) for k in range(4)]
    for k in range(3):
        acc = column_set(acc, 32 + k, sums[k])
    square[0:1, :] = sum(
        jnp.sum(wout[t].astype(F32) * dw[0, t], axis=0, keepdims=True) for t in range(parts)
    )
    products = jnp.concatenate(
        [
            jnp.transpose(square[:, i * LANES : (i + 1) * LANES])[:, 0:1]
            for i in range(width // LANES)
        ]
    )
    acc = column_set(acc, 35, products / chan[:, 3:4] + chan[:, 2:3] * sums[3])
    hidden_sums = jnp.sum(bin_acc[...], axis=1, keepdims=True)
    for k in range(shard // local):
        starts = [t * shard + k * local for t in range(parts)]
        acc = column_set(acc, 36 + k, jnp.concatenate([hidden_sums[i : i + local] for i in starts]))
    col_mine[...] = acc.reshape(parts, local, LANES)
    col_peer[mine] = col_mine[...]
    col_copies = [remote(col_mine, col_peer.at[mine], p) for p in beside]

    dw_near.wait()
    for copy in dw_copies:
        copy.wait()
    near(dw_peer, dw).wait()
    slabs = [dw[:, :, i * slab : (i + 1) * slab, :] for i in range(groups)]
    dw_sum[...] = sum(slabs[1:], slabs[0])
    dw_tensor[me] = dw_sum[:, me]
    dw_copies = [remote(dw_sum.at[:, p["tensor"]], dw_tensor.at[me], p) for p in across]
    arrived(col_copies)
    col_sum[...] = sum((col_peer[i] for i in range(1, groups)), col_peer[0])
    col_tensor[me] = col_sum[me]
    col_copies = [remote(col_sum.at[p["tensor"]], col_tensor.at[me], p) for p in across]
    arrived(dw_copies)
    dw_done[...] = sum((dw_tensor[i] for i in range(1, parts)), dw_tensor[0])
    dw_near = near(dw_done, dw_own.at[:, my_slab, :])
    dw_copies = [remote(dw_done, dw_own.at[:, my_slab, :], p) for p in beside]
    arrived(col_copies)
    cols = sum((col_tensor[i] for i in range(1, parts)), col_tensor[0])
    gdt = lag_grads(cols, steps, a_log, a_imag, coefs, g_alog, g_aimag, [g_height, g_width])
    for j in range(2):
        cols = column_set(cols, j, gdt[j])
    square[0:local, 0:LANES] = cols
    row_own[...] = jnp.transpose(square[:, 0:LANES])

    arrived(dw_copies)
    dw_near.wait()
    arrived(res_copies)
    res_mine.wait()

    @pl.loop(0, local // GROUP)
    def _(q):
        for copy in gx_copies(q):
            copy.wait()

    for copy in sent:
        copy.wait_send()


def block(parts, groups, args):
    x, size = args[0], args[2]
    local, pixels = x.shape
    pix = pixels // parts
    width = local * parts
    w_in = args[12]
    shard = w_in.shape[1]
    ff = shard * parts
    slab = shard // groups
    tiles = local // GROUP
    states = args[4].shape[1]
    shape = jax.ShapeDtypeStruct
    vmem = pl.BlockSpec(memory_space=pltpu.VMEM)
    hbm = pl.BlockSpec(memory_space=pl.ANY)
    in_specs = [hbm, hbm] + [vmem] * 10 + [hbm, vmem, hbm, vmem, vmem]
    outs = [
        (shape((parts, local, pix), BF16), hbm),
        (shape((parts, local, pix), BF16), hbm),
        (shape((2, shard, width), F32), hbm),
        (shape((local, states), F32), vmem),
        (shape((local, states), F32), vmem),
        (shape((2, local, states), F32), vmem),
        (shape((2, local, states), F32), vmem),
        (shape((LANES, LANES), F32), vmem),
        (shape((parts, local, pix), BF16), hbm),
        (shape((ff, pix), BF16), hbm),
        (shape((ff, pix), BF16), hbm),
        (shape((parts, local, pix), BF16), hbm),
        (shape((2, parts, shard, width), F32), hbm),
    ]
    remotes = 9 * (parts - 1) + 5 * (groups - 1)
    dma = pltpu.SemaphoreType.DMA
    scratch = [
        pltpu.VMEM((parts, local, pix), BF16),
        pltpu.VMEM((parts, local, pix), BF16),
        pltpu.VMEM((parts, local, STEP), BF16),
        pltpu.VMEM((pix, LANES), F32),
        pltpu.VMEM((tiles, pix, LANES), F32),
        pltpu.VMEM((CROP, CROP, 8, LANES), F32),
        pltpu.VMEM((CROP, CROP, 8, LANES), F32),
        pltpu.VMEM((4, 2 * CROP, 8, LANES), F32),
        pltpu.VMEM((local, LANES), F32),
        pltpu.VMEM((parts, local, LANES), F32),
        pltpu.VMEM((tiles, LANES, LANES), F32),
        pltpu.VMEM((tiles, LANES, LANES), F32),
        pltpu.VMEM((8, shard), F32),
        pltpu.VMEM((parts, 8, shard), F32),
        pltpu.VMEM((ff, LANES), F32),
        pltpu.VMEM((width, LANES), F32),
        pltpu.VMEM((LANES, width), F32),
        pltpu.VMEM((width, ff), BF16),
        pltpu.VMEM((ff, width), BF16),
        pltpu.VMEM((parts, shard, width), BF16),
        pltpu.VMEM((width, ff), BF16),
        pltpu.VMEM((ff, STEP), BF16),
        pltpu.VMEM((ff, STEP), BF16),
        pltpu.VMEM((ff, STEP), BF16),
        pltpu.VMEM((parts, local, STEP), BF16),
        pltpu.VMEM((2, parts, shard, width), F32),
        pltpu.VMEM((2, parts, slab, width), F32),
        pltpu.VMEM((parts, 2, slab, width), F32),
        pltpu.VMEM((2, slab, width), F32),
        pltpu.VMEM((ff, LANES), F32),
        pltpu.VMEM((4, width, LANES), F32),
        pltpu.VMEM((parts, local, LANES), F32),
        pltpu.VMEM((groups, parts, local, LANES), F32),
        pltpu.VMEM((parts, local, LANES), F32),
        pltpu.VMEM((parts, local, LANES), F32),
        dma((remotes,)),
        dma((remotes,)),
        dma((8,)),
        dma((parts,)),
        dma((parts,)),
        dma,
        dma,
        dma((tiles, parts - 1)),
        dma((tiles, parts - 1)),
        dma((tiles,)),
    ]
    return pl.pallas_call(
        functools.partial(block_kernel, parts, groups),
        out_shape=[o[0] for o in outs],
        in_specs=in_specs,
        out_specs=[o[1] for o in outs],
        scratch_shapes=scratch,
        compiler_params=pltpu.CompilerParams(
            collective_id=0, has_side_effects=True, vmem_limit_bytes=VMEM
        ),
        name="block",
    )(*args)


def finish_kernel(res_ref, g_ref, go_ref, result_ref, grad_ref):
    result_ref[...] = res_ref[0]
    grad_ref[...] = go_ref[...].astype(F32) + g_ref[0].astype(F32)


def finish(res_own, g_own, grad_out):
    parts, local, pix = g_own.shape
    part = pl.BlockSpec((1, GROUP, pix), lambda s, q: (s, q, 0))
    tile = pl.BlockSpec((GROUP, pix), lambda s, q: (q, s))
    return pl.pallas_call(
        finish_kernel,
        grid=(parts, local // GROUP),
        out_shape=(
            jax.ShapeDtypeStruct(grad_out.shape, BF16),
            jax.ShapeDtypeStruct(grad_out.shape, F32),
        ),
        in_specs=[part, part, tile],
        out_specs=(tile, tile),
        compiler_params=pltpu.CompilerParams(vmem_limit_bytes=32 << 20),
        name="finish",
    )(res_own, g_own, grad_out)


def per_device(
    parts,
    dp_size,
    inputs,
    crop_size,
    crop_offset,
    a_log,
    a_imag,
    c_height,
    c_width,
    log_dt,
    skip_gain,
    ln_gain,
    ln_bias,
    w_in,
    b_in,
    w_out,
    b_out,
    layer_scale,
    grad_out,
):
    local = inputs.shape[0]
    canvases = crop_size.shape[0]
    groups = min(dp_size, 8)
    args = (
        inputs,
        grad_out,
        crop_size.reshape(canvases, 8),
        crop_offset.reshape(canvases, 8),
        a_log,
        a_imag,
        c_height,
        c_width,
        log_dt,
        skip_gain[None],
        ln_gain[None],
        ln_bias[None],
        w_in,
        b_in[None],
        w_out,
        b_out[None],
        layer_scale[None],
    )
    out = block(parts, groups, args)
    result, grad_inputs = finish(out[0], out[1], grad_out)
    sums = tuple(out[2:8])
    if dp_size > groups:
        teams = [[r + groups * g for g in range(dp_size // groups)] for r in range(groups)]
        sums = lax.psum(sums, "dp", axis_index_groups=teams)
    dw, g_alog, g_aimag, g_height, g_width, rows = sums
    rows = rows[:, :local]
    return (
        result,
        grad_inputs,
        g_alog,
        g_aimag,
        g_height,
        g_width,
        rows[0:2],
        rows[2 * CROP],
        rows[33],
        rows[34],
        jnp.transpose(dw[1]),
        rows[36 : 36 + b_in.shape[0] // local].reshape(b_in.shape),
        dw[0],
        rows[32],
        rows[35],
    )


def solution(mesh):
    in_specs = (
        P("tensor", "dp"),
        P("dp", None, None),
        P("dp", None, None),
        P("tensor", None),
        P("tensor", None),
        P(None, "tensor", None),
        P(None, "tensor", None),
        P(None, "tensor"),
        P("tensor"),
        P(),
        P(),
        P(None, "tensor"),
        P("tensor"),
        P("tensor", None),
        P(),
        P(),
        P("tensor", "dp"),
    )
    out_specs = (
        P("tensor", "dp"),
        P("tensor", "dp"),
        P("tensor", None),
        P("tensor", None),
        P(None, "tensor", None),
        P(None, "tensor", None),
        P(None, "tensor"),
        P("tensor"),
        P("tensor"),
        P("tensor"),
        P(None, "tensor"),
        P("tensor"),
        P("tensor", None),
        P("tensor"),
        P("tensor"),
    )
    return jax.shard_map(
        functools.partial(per_device, mesh.shape["tensor"], mesh.shape["dp"]),
        mesh=mesh,
        in_specs=in_specs,
        out_specs=out_specs,
        check_vma=False,
    )
```

time: 3660 us -> 533 us (0.15)
  waiting for transfers between devices: 2520 us -> 0 us
  matrix products: 582 us -> 0 us
  Pallas kernels: 0 us -> 493 us
  local copies, waits for them, and re-layouts: 344 us -> 35.4 us
  other arithmetic: 179 us -> 0 us
    psum x3 -> x0, waiting for transfers between devices: 1250 us -> none  [the longest x1 1210 us: per_device(): grad_normed = lax.psum(grad_normed_part, 'tensor')]
    all_gather x2 -> x0, waiting for transfers between devices: 656 us -> none  [the longest x1 328 us: per_device(): grad_full = lax.all_gather(grad_branch, 'tensor', axis=0, tiled=True)]
    unnamed x7 -> x0, waiting for transfers between devices: 623 us -> none
    dot_general x16 -> x0, matrix products: 582 us -> none  [the longest x3 218 us: mixer_first(): jnp.einsum('chk,cnakbw->cnahbw', kern_height, masked, precision=lax.Preci...]
    pallas_call x0 -> x2, Pallas kernels: none -> 493 us  [the longest x1 486 us: block(): pl.pallas_call(functools.partial(block_kernel, parts, groups), out_shape=...]
    reduce_sum x8 -> x0, other arithmetic: 107 us -> none  [the longest x1 32.8 us: per_device(): mean_one = jnp.mean(grad_scaled, axis=0, keepdims=True)]
    unnamed x123 -> x15, local copies, waits for them, and re-layouts: 105 us -> 20.4 us
    dot_general x4 -> x0, local copies, waits for them, and re-layouts: 60.5 us -> none  [the longest x1 30.4 us: mixer_first(): jnp.einsum('chk,cnakbw->cnahbw', kern_height, masked, precision=lax.Preci...]
  transfers between devices with their start and end apart: 6 -> 0, of which waited for: 5 -> 0; matrix products, arithmetic and copies ran while one was open for 16% -> 0% of each run, Pallas kernels for 0% -> 0%
where the time goes in v2:
time: 533 us; the launch traced here: 529 us
  Pallas kernels  493 us (92%)
  local copies, waits for them, and re-layouts  35.4 us (7%)
    pallas_call x1, Pallas kernels, block(): pl.pallas_call(functools.partial(block_kernel, parts, groups), out_shape=...  486 us
    unnamed x15, local copies, waits for them, and re-layouts  20.4 us

profile of v2, /device:TPU:24, one launch (start us, length us, event | category | flops | bytes accessed | tf_op | source)
XLA Modules:
  0.0 529.4 jit_solution(2858279880090666487)
XLA Ops:
  0.6 1.2 broadcast_in_dim.19.ln_gain
  1.9 1.2 broadcast_in_dim.20.ln_bias
  3.1 1.2 broadcast_in_dim.21.b_in
  4.4 1.2 broadcast_in_dim.22.b_out
  5.6 1.3 broadcast_in_dim.23.layer_scale
  6.9 1.4 copy.43.size_ref
  8.2 1.4 copy.44.offset_ref
  9.6 1.5 copy.45.a_log
  11.1 1.5 copy.46.a_imag
  12.5 1.6 copy.47.c_height
  14.1 1.6 copy.48.c_width
  15.7 486.3 %block.1 = (bf16[4,96,6272]{2,1,0:T(8,128)(2,1)}, bf16[4,96,6272]{2,1,0:T(8,128)(2,1)}, f32[2,384,384]{2,1,0:T(8,128)}, f32[96,64]{1,0:T(8,128)}, f32[96,64]{1,0...) custom-call(bf16[96,25088]{1,0:T(8,128)(2,1)} %x.1, ...), custom_call_target="tpu_custom_call" | custom-call | tf_op jit(solution)/shard_map/block/pallas_call | solution.py:707
  502.0 1.2 slice.35
  503.2 0.7 slice.40
  503.9 1.4 slice_bitcast_fusion.2
  505.3 0.7 reshape.41
  505.9 1.5 copy.49
  507.4 1.5 copy.50
  508.9 1.6 copy.51
  510.5 1.6 copy.52
  512.1 2.1 slice_bitcast_fusion
  514.3 1.0 copy.53
  515.3 0.0 copy-start
  515.3 2.4 copy-done
  517.7 0.0 copy-start.1
  517.7 2.4 copy-done.1
  520.0 0.0 copy-start.2
  520.0 2.4 copy-done.2
  522.4 7.0 %finish.1 = (bf16[96,25088]{1,0:T(8,128)(2,1)}, f32[96,25088]{1,0:T(8,128)}) custom-call(bf16[4,96,6272]{2,1,0:T(8,128)(2,1)S(1)} %copy-done.1, bf16[4,96,6272]{2,1,0:T(8,128)(2,1)S(1)} %copy-done.2, bf16[96,25088]{1,0:T(8,128)(2,1)S(1)} %copy-done), custom_call_target="tpu_custom_call" | custom-call | tf_op jit(solution)/shard_map/finish/pallas_call | solution.py:729
Async XLA Ops:
  515.3 2.4 copy-start
  517.7 2.4 copy-start.1
  520.0 2.4 copy-start.2

commit v3 on v2

--- a/solution.py
+++ b/solution.py
@@ -148,7 +148,7 @@
     gk_height, gk_width, gskip = lax.fori_loop(
         0, 4, per_slot, ((zero,) * CROP, (zero,) * CROP, zero)
     )
-    gkern[q] = jnp.zeros((LANES, LANES), F32)
+    gkern[q] = jnp.zeros((32, LANES), F32)
     for row, v in enumerate((*gk_height, *gk_width, gskip)):
         gkern[q, pl.ds(row, 1), :] = jnp.sum(v, axis=0, keepdims=True)
     rows_to_lanes(grow.at[q], lambda off, v: put_tile(out, q, off, v))
@@ -172,24 +172,23 @@
     return jnp.where(lane == k, col, acc)
 
 
-def lag_kernels(steps, skip, a_log, a_imag, coefs):
-    acc = jnp.zeros((a_log.shape[0], LANES), F32)
+def lag_kernels(steps, a_log, a_imag, coefs, out):
+    local = a_log.shape[1]
     for j in range(2):
         _, _, waves = lag_waves(steps[j], a_log[...], a_imag[...])
         for l, (re, im) in enumerate(waves):
-            col = jnp.sum(coefs[j][0] * re - coefs[j][1] * im, axis=1, keepdims=True)
-            acc = column_set(acc, CROP * j + l, col)
-    return column_set(acc, 2 * CROP, skip)
-
-
-def lag_grads(cols, steps, a_log, a_imag, coefs, g_alog, g_aimag, g_coefs):
+            row = jnp.sum(coefs[j][0] * re - coefs[j][1] * im, axis=0, keepdims=True)
+            out[CROP * j + l : CROP * j + l + 1, 0:local] = row
+
+
+def lag_grads(rows, steps, a_log, a_imag, coefs, g_alog, g_aimag, g_coefs):
     ga, gi, gdt = 0.0, 0.0, []
     for j in range(2):
         rate, phase, waves = lag_waves(steps[j], a_log[...], a_imag[...])
         cre, cim = coefs[j][0], coefs[j][1]
         g_re = g_im = p = r = 0.0
         for l, (re, im) in enumerate(waves):
-            g = cols[:, CROP * j + l : CROP * j + l + 1]
+            g = rows[CROP * j + l : CROP * j + l + 1, 0 : a_log.shape[1]]
             g_re = g_re + g * re
             g_im = g_im - g * im
             if l:
@@ -199,7 +198,7 @@
         g_coefs[j][1] = g_im
         ga = ga + p * rate
         gi = gi + r * steps[j]
-        gdt.append(jnp.sum(p * rate + r * phase, axis=1, keepdims=True))
+        gdt.append(jnp.sum(p * rate + r * phase, axis=0, keepdims=True))
     g_alog[...] = ga
     g_aimag[...] = gi
     return gdt
@@ -258,15 +257,14 @@
     inner,
     mid,
     mask,
-    kern_mine,
-    kern_all,
+    small_mine,
+    small_all,
     kern,
     gkern,
-    bin_mine,
-    bin_all,
     bin_col,
     chan,
     square,
+    turned,
     win,
     win_t,
     wout,
@@ -277,14 +275,15 @@
     go_near,
     dw,
     dw_sum,
+    dw_low,
     dw_tensor,
     dw_done,
     bin_acc,
     vec,
-    col_mine,
-    col_peer,
-    col_sum,
-    col_tensor,
+    pack_mine,
+    pack_peer,
+    pack_sum,
+    pack_tensor,
     send,
     recv,
     own,
@@ -350,31 +349,28 @@
         return ref.at[:, pl.ds(pl.multiple_of(peer * pix, LANES), pix)]
 
     def to_owner(ref, out):
-        copies = [remote(pixels(ref, p["tensor"]), out.at[me], p) for p in across]
-        return copies, near(pixels(ref, me), out.at[me])
-
-    x_copies, x_near = to_owner(x, x_all)
+        return [remote(pixels(ref, p["tensor"]), out.at[me], p) for p in across]
+
     my_slab = pl.ds(pl.multiple_of(mine * slab, slab), slab)
     my_cols = pl.ds(pl.multiple_of(me * shard, LANES), shard)
+    w_copies = [remote(w_in.at[my_slab, :], win.at[my_slab, my_cols], p) for p in across]
+    w_copies += [remote(w_out.at[my_slab, :], wout.at[me, my_slab, :], p) for p in across]
     w_near = [
         near(w_in.at[my_slab, :], win.at[my_slab, my_cols]),
         near(w_out.at[my_slab, :], wout.at[me, my_slab, :]),
     ]
-    w_copies = [remote(w_in.at[my_slab, :], win.at[my_slab, my_cols], p) for p in across]
-    w_copies += [remote(w_out.at[my_slab, :], wout.at[me, my_slab, :], p) for p in across]
-
-    square[...] = jnp.zeros_like(square)
-    square[0:2, 0:local] = log_dt[...]
-    square[2:3, 0:local] = skip_gain[...]
-    turned = jnp.transpose(square[:, 0:LANES])
-    steps = [jnp.exp(turned[0:local, j : j + 1]) for j in range(2)]
+    steps = [jnp.exp(log_dt[j : j + 1, :]) for j in range(2)]
     coefs = [c_height, c_width]
-    kern_mine[...] = lag_kernels(steps, turned[0:local, 2:3], a_log, a_imag, coefs)
-    bin_mine[...] = jnp.broadcast_to(b_in[...], bin_mine.shape)
-    kern_all[me] = kern_mine[...]
-    bin_all[me] = bin_mine[...]
-    k_copies = [remote(kern_mine, kern_all.at[me], p) for p in across]
-    k_copies += [remote(bin_mine, bin_all.at[me], p) for p in across]
+    small_mine[...] = jnp.zeros_like(small_mine)
+    lag_kernels(steps, a_log, a_imag, coefs, small_mine)
+    small_mine[2 * CROP : 2 * CROP + 1, 0:local] = skip_gain[...].reshape(1, local)
+    biases = b_in[...].reshape(1, shard)
+    for i in range(shard // LANES):
+        small_mine[32 + i : 33 + i, :] = biases[:, i * LANES : (i + 1) * LANES]
+    small_all[me] = small_mine[...]
+    small_copies = [remote(small_mine, small_all.at[me], p) for p in across]
+    x_copies = to_owner(x, x_all)
+    x_near = near(pixels(x, me), x_all.at[me])
 
     for copy in w_near:
         copy.wait()
@@ -382,28 +378,31 @@
     w_copies = [remote(win.at[my_slab, :], win.at[my_slab, :], p) for p in beside]
     w_copies += [remote(wout.at[:, my_slab, :], wout.at[:, my_slab, :], p) for p in beside]
 
-    row = 0
-    for ref in (ln_gain, ln_bias, b_out, layer_scale):
-        square[row : row + 1, :] = ref[...]
-        row += 1
+    square[...] = jnp.zeros_like(square)
+    for row, ref in enumerate((ln_gain, ln_bias, b_out, layer_scale)):
+        square[row : row + 1, :] = ref[...].reshape(1, width)
     for i in range(width // LANES):
         chan[i * LANES : (i + 1) * LANES, :] = jnp.transpose(square[:, i * LANES : (i + 1) * LANES])
+    canvases = size_ref.shape[1]
+    square[0:8, 0:canvases] = offset_ref[...].astype(F32)
+    square[8:16, 0:canvases] = size_ref[...].astype(F32)
+    turned[...] = jnp.transpose(square[:, 0:LANES])
     at = pl.ds(pl.multiple_of(me * 8, 8), 8)
-    lo, extent = offset_ref[at, :], size_ref[at, :]
     for slot in range(4):
         for j in range(2):
             k = 2 * slot + j
-            low = jnp.broadcast_to(lo[:, k : k + 1], (8, LANES))
-            high = low + jnp.broadcast_to(extent[:, k : k + 1], (8, LANES))
+            low = jnp.broadcast_to(turned[at, k : k + 1], (8, LANES))
+            high = low + jnp.broadcast_to(turned[at, 8 + k : 9 + k], (8, LANES))
             for s in range(CROP):
                 mask[slot, CROP * j + s] = jnp.where((low <= s) & (s < high), 1.0, 0.0)
-    arrived(k_copies)
+    arrived(small_copies)
     for q in range(local // GROUP):
-        part = kern_all[:, q * GROUP : (q + 1) * GROUP, :].reshape(LANES, LANES)
-        kern[q] = jnp.transpose(part)
+        kern[q] = jnp.concatenate(
+            [small_all[t, 0:32, q * GROUP : (q + 1) * GROUP] for t in range(parts)], axis=1
+        )
     for t in range(parts):
         for i in range(shard // LANES):
-            block = jnp.broadcast_to(bin_all[t, 0:1, i * LANES : (i + 1) * LANES], (LANES, LANES))
+            block = jnp.broadcast_to(small_all[t, 32 + i : 33 + i, :], (LANES, LANES))
             bin_col[t * shard + i * LANES : t * shard + (i + 1) * LANES, :] = jnp.transpose(block)
     arrived(w_copies)
     for t in range(parts):
@@ -413,7 +412,7 @@
 
     arrived(x_copies)
     x_near.wait()
-    go_copies, go_own = to_owner(go, go_all)
+    go_copies = to_owner(go, go_all)
 
     @pl.loop(0, local // GROUP)
     def _(q):
@@ -428,9 +427,15 @@
             pltpu.make_async_copy(*p, sem.at[t]) for p, sem in zip(pair, (hid_sem, slope_sem))
         ]
 
-    def res_copy(j):
+    others = [p["tensor"] for p in across]
+
+    def res_chunk(j):
         lanes = pl.ds(pl.multiple_of(j * STEP, LANES), STEP)
-        return pltpu.make_async_copy(res_near, res.at[:, :, lanes], res_sem)
+        pairs = [(t, res) for t in others] + [(me, res_own)]
+        return [
+            pltpu.make_async_copy(res_near.at[t], ref.at[t, :, lanes], res_sem.at[i])
+            for i, (t, ref) in enumerate(pairs)
+        ]
 
     def low_of(off):
         normed, scale = norm(mixed[:, :, pl.ds(off, STEP)].reshape(width, STEP).astype(F32))
@@ -463,10 +468,12 @@
 
         @pl.when(j > 0)
         def _():
-            res_copy(j).wait()
+            for copy in res_chunk(j):
+                copy.wait()
 
         res_near[...] = out.reshape(parts, local, STEP)
-        res_copy(j).start()
+        for copy in res_chunk(j):
+            copy.start()
 
     for t in range(parts):
         for copy in hid_copy(t, 0, False):
@@ -474,26 +481,32 @@
         for copy in hid_copy(t, 0, True):
             copy.start()
 
-    res_copy(0).wait()
+    for copy in res_chunk(0):
+        copy.wait()
 
     arrived(go_copies)
-    go_own.wait()
     res_copies = [remote(res.at[p["tensor"]], res_own.at[me], p) for p in across]
-    res_mine = near(res.at[me], res_own.at[me])
 
     for ref in (dw, bin_acc, vec):
         ref[...] = jnp.zeros_like(ref)
 
-    def go_copy(j):
-        lanes = pl.ds(pl.multiple_of(j * STEP, LANES), STEP)
-        return pltpu.make_async_copy(go_all.at[:, :, lanes], go_near, go_sem)
-
-    go_copy(0).start()
+    def go_chunk(j):
+        off = pl.multiple_of(j * STEP, LANES)
+        mine_at = pl.ds(pl.multiple_of(me * pix + off, LANES), STEP)
+        sources = [(t, go_all.at[t, :, pl.ds(off, STEP)]) for t in others] + [(me, go.at[:, mine_at])]
+        return [
+            pltpu.make_async_copy(src, go_near.at[t], go_sem.at[i])
+            for i, (t, src) in enumerate(sources)
+        ]
+
+    for copy in go_chunk(0):
+        copy.start()
 
     @pl.loop(0, chunks)
     def _(j):
         off = pl.multiple_of(j * STEP, LANES)
-        go_copy(j).wait()
+        for copy in go_chunk(j):
+            copy.wait()
         grad = go_near[...].reshape(width, STEP).astype(F32)
         gb = (grad * chan[:, 3:4]).astype(BF16)
         vec[0] += fold(gb.astype(F32))
@@ -501,7 +514,8 @@
 
         @pl.when(j + 1 < chunks)
         def _():
-            go_copy(j + 1).start()
+            for copy in go_chunk(j + 1):
+                copy.start()
 
         normed, scale, low = low_of(off)
         for t in range(parts):
@@ -558,17 +572,22 @@
     @pl.loop(0, local // GROUP)
     def _(q):
         mix_bwd(q, x_all, rows, grow, kern, mask, inner, mid, mixed, gkern)
-        for copy in gx_copies(q):
-            copy.start()
-
-    for q in range(local // GROUP):
-        col_mine[:, q * GROUP : (q + 1) * GROUP, :] = jnp.transpose(gkern[q]).reshape(
-            parts, GROUP, LANES
+
+        @pl.when(q + 1 < local // GROUP)
+        def _():
+            for copy in gx_copies(q):
+                copy.start()
+
+    for t in range(parts):
+        lanes = slice(t * GROUP, (t + 1) * GROUP)
+        pack_mine[t] = jnp.zeros(pack_mine.shape[1:], F32)
+        pack_mine[t, 0:32, 0:local] = jnp.concatenate(
+            [gkern[q, 0:32, lanes] for q in range(local // GROUP)], axis=1
         )
-    acc = col_mine[...].reshape(width, LANES)
+    acc = jnp.zeros((width, LANES), F32)
     sums = [jnp.sum(vec[k], axis=1, keepdims=True) for k in range(4)]
     for k in range(3):
-        acc = column_set(acc, 32 + k, sums[k])
+        acc = column_set(acc, k, sums[k])
     square[0:1, :] = sum(
         jnp.sum(wout[t].astype(F32) * dw[0, t], axis=0, keepdims=True) for t in range(parts)
     )
@@ -578,14 +597,16 @@
             for i in range(width // LANES)
         ]
     )
-    acc = column_set(acc, 35, products / chan[:, 3:4] + chan[:, 2:3] * sums[3])
+    acc = column_set(acc, 3, products / chan[:, 3:4] + chan[:, 2:3] * sums[3])
     hidden_sums = jnp.sum(bin_acc[...], axis=1, keepdims=True)
     for k in range(shard // local):
         starts = [t * shard + k * local for t in range(parts)]
-        acc = column_set(acc, 36 + k, jnp.concatenate([hidden_sums[i : i + local] for i in starts]))
-    col_mine[...] = acc.reshape(parts, local, LANES)
-    col_peer[mine] = col_mine[...]
-    col_copies = [remote(col_mine, col_peer.at[mine], p) for p in beside]
+        acc = column_set(acc, 4 + k, jnp.concatenate([hidden_sums[i : i + local] for i in starts]))
+    for t in range(parts):
+        square[0:local, 0:LANES] = acc[t * local : (t + 1) * local]
+        pack_mine[t, 32:40, :] = jnp.transpose(square[:, 0:LANES])[0:8]
+    pack_peer[mine] = pack_mine[...]
+    pack_copies = [remote(pack_mine, pack_peer.at[mine], p) for p in beside]
 
     dw_near.wait()
     for copy in dw_copies:
@@ -593,28 +614,29 @@
     near(dw_peer, dw).wait()
     slabs = [dw[:, :, i * slab : (i + 1) * slab, :] for i in range(groups)]
     dw_sum[...] = sum(slabs[1:], slabs[0])
-    dw_tensor[me] = dw_sum[:, me]
-    dw_copies = [remote(dw_sum.at[:, p["tensor"]], dw_tensor.at[me], p) for p in across]
-    arrived(col_copies)
-    col_sum[...] = sum((col_peer[i] for i in range(1, groups)), col_peer[0])
-    col_tensor[me] = col_sum[me]
-    col_copies = [remote(col_sum.at[p["tensor"]], col_tensor.at[me], p) for p in across]
+    dw_low[...] = dw_sum[...].astype(BF16)
+    dw_copies = [remote(dw_low.at[:, t], dw_tensor.at[me], p) for t, p in zip(others, across)]
+    arrived(pack_copies)
+    pack_sum[...] = sum((pack_peer[i] for i in range(1, groups)), pack_peer[0])
+    pack_tensor[me] = pack_sum[me]
+    pack_copies = [remote(pack_sum.at[t], pack_tensor.at[me], p) for t, p in zip(others, across)]
+    for copy in gx_copies(local // GROUP - 1):
+        copy.start()
+
     arrived(dw_copies)
-    dw_done[...] = sum((dw_tensor[i] for i in range(1, parts)), dw_tensor[0])
+    dw_done[...] = sum((dw_tensor[t].astype(F32) for t in others), dw_sum[:, me])
     dw_near = near(dw_done, dw_own.at[:, my_slab, :])
     dw_copies = [remote(dw_done, dw_own.at[:, my_slab, :], p) for p in beside]
-    arrived(col_copies)
-    cols = sum((col_tensor[i] for i in range(1, parts)), col_tensor[0])
-    gdt = lag_grads(cols, steps, a_log, a_imag, coefs, g_alog, g_aimag, [g_height, g_width])
+    arrived(pack_copies)
+    total = sum((pack_tensor[i] for i in range(1, parts)), pack_tensor[0])
+    gdt = lag_grads(total, steps, a_log, a_imag, coefs, g_alog, g_aimag, [g_height, g_width])
+    row_own[...] = total
     for j in range(2):
-        cols = column_set(cols, j, gdt[j])
-    square[0:local, 0:LANES] = cols
-    row_own[...] = jnp.transpose(square[:, 0:LANES])
+        row_own[29 + j : 30 + j, 0:local] = gdt[j]
 
     arrived(dw_copies)
     dw_near.wait()
     arrived(res_copies)
-    res_mine.wait()
 
     @pl.loop(0, local // GROUP)
     def _(q):
@@ -635,7 +657,7 @@
     ff = shard * parts
     slab = shard // groups
     tiles = local // GROUP
-    states = args[4].shape[1]
+    states = args[4].shape[0]
     shape = jax.ShapeDtypeStruct
     vmem = pl.BlockSpec(memory_space=pltpu.VMEM)
     hbm = pl.BlockSpec(memory_space=pl.ANY)
@@ -644,18 +666,18 @@
         (shape((parts, local, pix), BF16), hbm),
         (shape((parts, local, pix), BF16), hbm),
         (shape((2, shard, width), F32), hbm),
-        (shape((local, states), F32), vmem),
-        (shape((local, states), F32), vmem),
-        (shape((2, local, states), F32), vmem),
-        (shape((2, local, states), F32), vmem),
-        (shape((LANES, LANES), F32), vmem),
+        (shape((states, local), F32), vmem),
+        (shape((states, local), F32), vmem),
+        (shape((2, states, local), F32), vmem),
+        (shape((2, states, local), F32), vmem),
+        (shape((40, LANES), F32), vmem),
         (shape((parts, local, pix), BF16), hbm),
         (shape((ff, pix), BF16), hbm),
         (shape((ff, pix), BF16), hbm),
         (shape((parts, local, pix), BF16), hbm),
         (shape((2, parts, shard, width), F32), hbm),
     ]
-    remotes = 9 * (parts - 1) + 5 * (groups - 1)
+    remotes = 8 * (parts - 1) + 5 * (groups - 1)
     dma = pltpu.SemaphoreType.DMA
     scratch = [
         pltpu.VMEM((parts, local, pix), BF16),
@@ -666,15 +688,14 @@
         pltpu.VMEM((CROP, CROP, 8, LANES), F32),
         pltpu.VMEM((CROP, CROP, 8, LANES), F32),
         pltpu.VMEM((4, 2 * CROP, 8, LANES), F32),
-        pltpu.VMEM((local, LANES), F32),
-        pltpu.VMEM((parts, local, LANES), F32),
-        pltpu.VMEM((tiles, LANES, LANES), F32),
-        pltpu.VMEM((tiles, LANES, LANES), F32),
-        pltpu.VMEM((8, shard), F32),
-        pltpu.VMEM((parts, 8, shard), F32),
+        pltpu.VMEM((40, LANES), F32),
+        pltpu.VMEM((parts, 40, LANES), F32),
+        pltpu.VMEM((tiles, 32, LANES), F32),
+        pltpu.VMEM((tiles, 32, LANES), F32),
         pltpu.VMEM((ff, LANES), F32),
         pltpu.VMEM((width, LANES), F32),
         pltpu.VMEM((LANES, width), F32),
+        pltpu.VMEM((LANES, LANES), F32),
         pltpu.VMEM((width, ff), BF16),
         pltpu.VMEM((ff, width), BF16),
         pltpu.VMEM((parts, shard, width), BF16),
@@ -685,21 +706,22 @@
         pltpu.VMEM((parts, local, STEP), BF16),
         pltpu.VMEM((2, parts, shard, width), F32),
         pltpu.VMEM((2, parts, slab, width), F32),
-        pltpu.VMEM((parts, 2, slab, width), F32),
+        pltpu.VMEM((2, parts, slab, width), BF16),
+        pltpu.VMEM((parts, 2, slab, width), BF16),
         pltpu.VMEM((2, slab, width), F32),
         pltpu.VMEM((ff, LANES), F32),
         pltpu.VMEM((4, width, LANES), F32),
-        pltpu.VMEM((parts, local, LANES), F32),
-        pltpu.VMEM((groups, parts, local, LANES), F32),
-        pltpu.VMEM((parts, local, LANES), F32),
-        pltpu.VMEM((parts, local, LANES), F32),
+        pltpu.VMEM((parts, 40, LANES), F32),
+        pltpu.VMEM((groups, parts, 40, LANES), F32),
+        pltpu.VMEM((parts, 40, LANES), F32),
+        pltpu.VMEM((parts, 40, LANES), F32),
         dma((remotes,)),
         dma((remotes,)),
         dma((8,)),
         dma((parts,)),
         dma((parts,)),
-        dma,
-        dma,
+        dma((parts,)),
+        dma((parts,)),
         dma((tiles, parts - 1)),
         dma((tiles, parts - 1)),
         dma((tiles,)),
@@ -717,27 +739,90 @@
     )(*args)
 
 
-def finish_kernel(res_ref, g_ref, go_ref, result_ref, grad_ref):
+def finish_kernel(
+    res_ref,
+    g_ref,
+    go_ref,
+    dw,
+    g_alog,
+    g_aimag,
+    g_height,
+    g_width,
+    rows,
+    result_ref,
+    grad_ref,
+    alog_out,
+    aimag_out,
+    height_out,
+    width_out,
+    dt_out,
+    skip_out,
+    gain_out,
+    bias_out,
+    win_out,
+    bin_out,
+    wout_out,
+    bout_out,
+    scale_out,
+):
     result_ref[...] = res_ref[0]
     grad_ref[...] = go_ref[...].astype(F32) + g_ref[0].astype(F32)
 
-
-def finish(res_own, g_own, grad_out):
+    @pl.when((pl.program_id(0) == 0) & (pl.program_id(1) == 0))
+    def _():
+        alog_out[...] = g_alog[...]
+        aimag_out[...] = g_aimag[...]
+        height_out[...] = g_height[...]
+        width_out[...] = g_width[...]
+        local = skip_out.shape[0]
+        dt_out[...] = rows[29:31, 0:local]
+        singles = ((skip_out, 28), (gain_out, 33), (bias_out, 34), (bout_out, 32), (scale_out, 35))
+        for out, k in singles:
+            out[...] = rows[k : k + 1, 0:local].reshape(local)
+        count = bin_out.shape[0] // local
+        bin_out[...] = jnp.concatenate(
+            [rows[36 + k : 37 + k, 0:local] for k in range(count)], axis=1
+        ).reshape(bin_out.shape)
+        win_out[...] = jnp.transpose(dw[1])
+        wout_out[...] = dw[0]
+
+
+def finish(res_own, g_own, grad_out, sums):
     parts, local, pix = g_own.shape
+    dw, g_alog, _, g_height, _, _ = sums
     part = pl.BlockSpec((1, GROUP, pix), lambda s, q: (s, q, 0))
     tile = pl.BlockSpec((GROUP, pix), lambda s, q: (q, s))
+
+    def whole(a):
+        return pl.BlockSpec(a.shape, lambda s, q: (0,) * len(a.shape))
+
+    shape = jax.ShapeDtypeStruct
+    line = shape((local,), F32)
+    small = (
+        g_alog,
+        g_alog,
+        g_height,
+        g_height,
+        shape((2, local), F32),
+        line,
+        line,
+        line,
+        shape((dw.shape[2], dw.shape[1]), F32),
+        shape((dw.shape[1],), F32),
+        shape(dw.shape[1:], F32),
+        line,
+        line,
+    )
+    small = tuple(shape(a.shape, F32) for a in small)
     return pl.pallas_call(
         finish_kernel,
         grid=(parts, local // GROUP),
-        out_shape=(
-            jax.ShapeDtypeStruct(grad_out.shape, BF16),
-            jax.ShapeDtypeStruct(grad_out.shape, F32),
-        ),
-        in_specs=[part, part, tile],
-        out_specs=(tile, tile),
-        compiler_params=pltpu.CompilerParams(vmem_limit_bytes=32 << 20),
+        out_shape=(shape(grad_out.shape, BF16), shape(grad_out.shape, F32)) + small,
+        in_specs=[part, part, tile] + [whole(a) for a in sums],
+        out_specs=(tile, tile) + tuple(whole(a) for a in small),
+        compiler_params=pltpu.CompilerParams(vmem_limit_bytes=VMEM),
         name="finish",
-    )(res_own, g_own, grad_out)
+    )(res_own, g_own, grad_out, *sums)
 
 
 def per_device(
@@ -761,52 +846,41 @@
     layer_scale,
     grad_out,
 ):
-    local = inputs.shape[0]
     canvases = crop_size.shape[0]
     groups = min(dp_size, 8)
     args = (
         inputs,
         grad_out,
-        crop_size.reshape(canvases, 8),
-        crop_offset.reshape(canvases, 8),
-        a_log,
-        a_imag,
-        c_height,
-        c_width,
+        jnp.transpose(crop_size.reshape(canvases, 8)),
+        jnp.transpose(crop_offset.reshape(canvases, 8)),
+        jnp.transpose(a_log),
+        jnp.transpose(a_imag),
+        jnp.transpose(c_height, (0, 2, 1)),
+        jnp.transpose(c_width, (0, 2, 1)),
         log_dt,
-        skip_gain[None],
-        ln_gain[None],
-        ln_bias[None],
+        skip_gain,
+        ln_gain,
+        ln_bias,
         w_in,
-        b_in[None],
+        b_in,
         w_out,
-        b_out[None],
-        layer_scale[None],
+        b_out,
+        layer_scale,
     )
     out = block(parts, groups, args)
-    result, grad_inputs = finish(out[0], out[1], grad_out)
     sums = tuple(out[2:8])
     if dp_size > groups:
         teams = [[r + groups * g for g in range(dp_size // groups)] for r in range(groups)]
         sums = lax.psum(sums, "dp", axis_index_groups=teams)
-    dw, g_alog, g_aimag, g_height, g_width, rows = sums
-    rows = rows[:, :local]
+    done = finish(out[0], out[1], grad_out, sums)
     return (
-        result,
-        grad_inputs,
-        g_alog,
-        g_aimag,
-        g_height,
-        g_width,
-        rows[0:2],
-        rows[2 * CROP],
-        rows[33],
-        rows[34],
-        jnp.transpose(dw[1]),
-        rows[36 : 36 + b_in.shape[0] // local].reshape(b_in.shape),
-        dw[0],
-        rows[32],
-        rows[35],
+        done[0],
+        done[1],
+        jnp.transpose(done[2]),
+        jnp.transpose(done[3]),
+        jnp.transpose(done[4], (0, 2, 1)),
+        jnp.transpose(done[5], (0, 2, 1)),
+        *done[6:],
     )
 
 

time: 533 us -> 456 us (0.86)
  Pallas kernels: 493 us -> 454 us
  local copies, waits for them, and re-layouts: 35.4 us -> 0 us
    pallas_call x1, Pallas kernels: 486 us -> 439 us  [block(): pl.pallas_call(functools.partial(block_kernel, parts, groups), out_shape=...]
    unnamed x15 -> x0, local copies, waits for them, and re-layouts: 20.4 us -> none
    pallas_call x1, Pallas kernels: 7.02 us -> 15.5 us  [finish(): pl.pallas_call(finish_kernel, grid=(parts, local // GROUP), out_shape=(sh...]
    broadcast_in_dim x5 -> x0, local copies, waits for them, and re-layouts: 6.23 us -> none  [the longest x1 1.27 us: per_device(): layer_scale[None]]
where the time goes in v3:
time: 456 us; the launch traced here: 455 us
  Pallas kernels  454 us (100%)
    pallas_call x1, Pallas kernels, block(): pl.pallas_call(functools.partial(block_kernel, parts, groups), out_shape=...  439 us
    pallas_call x1, Pallas kernels, finish(): pl.pallas_call(finish_kernel, grid=(parts, local // GROUP), out_shape=(sh...  15.5 us

profile of v3, /device:TPU:24, one launch (start us, length us, event | category | flops | bytes accessed | tf_op | source)
XLA Modules:
  0.0 454.9 jit_solution(17138008002873261122)
XLA Ops:
  0.7 438.6 %block.1 = (bf16[4,96,6272]{2,1,0:T(8,128)(2,1)}, bf16[4,96,6272]{2,1,0:T(8,128)(2,1)}, f32[2,384,384]{2,1,0:T(8,128)}, f32[64,96]{1,0:T(8,128)}, f32[64,96]{1,0...) custom-call(bf16[96,25088]{1,0:T(8,128)(2,1)} %x.1, ...), custom_call_target="tpu_custom_call" | custom-call | tf_op jit(solution)/shard_map/block/pallas_call | solution.py:729
  439.2 15.5 %finish.1 = (bf16[96,25088]{1,0:T(8,128)(2,1)}, f32[96,25088]{1,0:T(8,128)}, f32[64,96]{1,0:T(8,128)}, f32[64,96]{1,0:T(8,128)}, f32[2,64,96]{2,1,0:T(8,128)}, /...) custom-call(bf16[4,96,6272]{2,1,0:T(8,128)(2,1)} %get-tuple-element., ...), custom_call_target="tpu_custom_call" | custom-call | tf_op jit(solution)/shard_map/finish/pallas_call | solution.py:817

commit v4 on v3

--- a/solution.py
+++ b/solution.py
@@ -151,7 +151,12 @@
     gkern[q] = jnp.zeros((32, LANES), F32)
     for row, v in enumerate((*gk_height, *gk_width, gskip)):
         gkern[q, pl.ds(row, 1), :] = jnp.sum(v, axis=0, keepdims=True)
-    rows_to_lanes(grow.at[q], lambda off, v: put_tile(out, q, off, v))
+
+    @pl.loop(0, rows.shape[0] // STEP)
+    def _(j):
+        off = pl.multiple_of(j * STEP, LANES)
+        turned = jnp.transpose(grow[q, pl.ds(off, STEP), :])
+        put_tile(out, q, off, (tile_of(out, q, off).astype(F32) + turned).astype(BF16))
 
 
 def lag_waves(step, a_log, a_imag):
@@ -287,6 +292,8 @@
     send,
     recv,
     own,
+    hop_send,
+    hop_recv,
     hid_sem,
     slope_sem,
     go_sem,
@@ -352,29 +359,77 @@
         return [remote(pixels(ref, p["tensor"]), out.at[me], p) for p in across]
 
     my_slab = pl.ds(pl.multiple_of(mine * slab, slab), slab)
-    my_cols = pl.ds(pl.multiple_of(me * shard, LANES), shard)
-    w_copies = [remote(w_in.at[my_slab, :], win.at[my_slab, my_cols], p) for p in across]
-    w_copies += [remote(w_out.at[my_slab, :], wout.at[me, my_slab, :], p) for p in across]
-    w_near = [
-        near(w_in.at[my_slab, :], win.at[my_slab, my_cols]),
-        near(w_out.at[my_slab, :], wout.at[me, my_slab, :]),
-    ]
     steps = [jnp.exp(log_dt[j : j + 1, :]) for j in range(2)]
     coefs = [c_height, c_width]
-    small_mine[...] = jnp.zeros_like(small_mine)
-    lag_kernels(steps, a_log, a_imag, coefs, small_mine)
-    small_mine[2 * CROP : 2 * CROP + 1, 0:local] = skip_gain[...].reshape(1, local)
-    biases = b_in[...].reshape(1, shard)
-    for i in range(shard // LANES):
-        small_mine[32 + i : 33 + i, :] = biases[:, i * LANES : (i + 1) * LANES]
+
+    partner = {"tensor": me + 1 - 2 * lax.rem(me, 2)}
+    inner_device = {"tensor": jnp.where(me < 2, 2, 1)}
+    is_inner = (me == 1) | (me == 2)
+    other_half = 2 - 2 * (me // 2)
+
+    def cols_of(t):
+        return pl.ds(pl.multiple_of(t * shard, LANES), shard)
+
+    def pieces(t):
+        return [
+            (win.at[my_slab, cols_of(t)], win.at[my_slab, cols_of(t)]),
+            (wout.at[t, my_slab, :], wout.at[t, my_slab, :]),
+            (small_all.at[t], small_all.at[t]),
+        ]
+
+    def hop(i, k, pair, peer, way):
+        return pltpu.make_async_remote_copy(
+            src_ref=pair[0],
+            dst_ref=pair[1],
+            send_sem=hop_send.at[way, i],
+            recv_sem=hop_recv.at[k, i],
+            device_id=peer,
+            device_id_type=MESH,
+        )
+
+    first_hops = []
+    slabs = [w_in.at[my_slab, :], w_out.at[my_slab, :], small_mine]
+    for i in range(3):
+        if i == 2:
+            small_mine[...] = jnp.zeros_like(small_mine)
+            lag_kernels(steps, a_log, a_imag, coefs, small_mine)
+            small_mine[2 * CROP : 2 * CROP + 1, 0:local] = skip_gain[...].reshape(1, local)
+            biases = b_in[...].reshape(1, shard)
+            for j in range(shard // LANES):
+                small_mine[32 + j : 33 + j, :] = biases[:, j * LANES : (j + 1) * LANES]
+        pair = (slabs[i], pieces(me)[i][1])
+        first_hops.append(hop(i, 0, pair, partner, 0))
+        first_hops.append(hop(i, 1 + lax.rem(me, 2), pair, inner_device, 1))
+        for copy in first_hops[-2:]:
+            copy.start()
+    w_near = [near(slabs[i], pieces(me)[i][1]) for i in range(2)]
     small_all[me] = small_mine[...]
-    small_copies = [remote(small_mine, small_all.at[me], p) for p in across]
+
+    def handed_on(k):
+        found = pieces(other_half + k)
+        return [hop(i, 1 + k, found[i], partner, 2 + k) for i in range(3)]
+
+    @pl.when(is_inner)
+    def _():
+        for k in range(2):
+            for copy in handed_on(k):
+                copy.wait_recv()
+            for copy in handed_on(k):
+                copy.start()
+
     x_copies = to_owner(x, x_all)
     x_near = near(pixels(x, me), x_all.at[me])
 
+    @pl.when(jnp.logical_not(is_inner))
+    def _():
+        for k in range(2):
+            for copy in handed_on(k):
+                copy.wait_recv()
+
     for copy in w_near:
         copy.wait()
-    arrived(w_copies)
+    for copy in first_hops[::2]:
+        copy.wait_recv()
     w_copies = [remote(win.at[my_slab, :], win.at[my_slab, :], p) for p in beside]
     w_copies += [remote(wout.at[:, my_slab, :], wout.at[:, my_slab, :], p) for p in beside]
 
@@ -395,7 +450,6 @@
             high = low + jnp.broadcast_to(turned[at, 8 + k : 9 + k], (8, LANES))
             for s in range(CROP):
                 mask[slot, CROP * j + s] = jnp.where((low <= s) & (s < high), 1.0, 0.0)
-    arrived(small_copies)
     for q in range(local // GROUP):
         kern[q] = jnp.concatenate(
             [small_all[t, 0:32, q * GROUP : (q + 1) * GROUP] for t in range(parts)], axis=1
@@ -552,6 +606,11 @@
         remote(dw.at[:, :, slab_of(p), :], dw_peer.at[:, :, my_slab, :], p) for p in beside
     ]
 
+    back = [near(go_all.at[t], mixed.at[t]) for t in others]
+    back.append(near(pixels(go, me), mixed.at[me]))
+    for copy in back:
+        copy.wait()
+
     def gx_tile(q):
         return pl.ds(pl.multiple_of(q * GROUP, GROUP), GROUP)
 
@@ -612,8 +671,8 @@
     for copy in dw_copies:
         copy.wait()
     near(dw_peer, dw).wait()
-    slabs = [dw[:, :, i * slab : (i + 1) * slab, :] for i in range(groups)]
-    dw_sum[...] = sum(slabs[1:], slabs[0])
+    terms = [dw[:, :, i * slab : (i + 1) * slab, :] for i in range(groups)]
+    dw_sum[...] = sum(terms[1:], terms[0])
     dw_low[...] = dw_sum[...].astype(BF16)
     dw_copies = [remote(dw_low.at[:, t], dw_tensor.at[me], p) for t, p in zip(others, across)]
     arrived(pack_copies)
@@ -643,8 +702,14 @@
         for copy in gx_copies(q):
             copy.wait()
 
-    for copy in sent:
+    for copy in sent + first_hops:
         copy.wait_send()
+
+    @pl.when(is_inner)
+    def _():
+        for k in range(2):
+            for copy in handed_on(k):
+                copy.wait_send()
 
 
 def block(parts, groups, args):
@@ -677,7 +742,7 @@
         (shape((parts, local, pix), BF16), hbm),
         (shape((2, parts, shard, width), F32), hbm),
     ]
-    remotes = 8 * (parts - 1) + 5 * (groups - 1)
+    remotes = 5 * (parts - 1) + 5 * (groups - 1)
     dma = pltpu.SemaphoreType.DMA
     scratch = [
         pltpu.VMEM((parts, local, pix), BF16),
@@ -717,7 +782,9 @@
         pltpu.VMEM((parts, 40, LANES), F32),
         dma((remotes,)),
         dma((remotes,)),
-        dma((8,)),
+        dma((10,)),
+        dma((4, 3)),
+        dma((3, 3)),
         dma((parts,)),
         dma((parts,)),
         dma((parts,)),
@@ -739,90 +806,100 @@
     )(*args)
 
 
-def finish_kernel(
-    res_ref,
-    g_ref,
-    go_ref,
-    dw,
-    g_alog,
-    g_aimag,
-    g_height,
-    g_width,
-    rows,
-    result_ref,
-    grad_ref,
-    alog_out,
-    aimag_out,
-    height_out,
-    width_out,
-    dt_out,
-    skip_out,
-    gain_out,
-    bias_out,
-    win_out,
-    bin_out,
-    wout_out,
-    bout_out,
-    scale_out,
-):
-    result_ref[...] = res_ref[0]
-    grad_ref[...] = go_ref[...].astype(F32) + g_ref[0].astype(F32)
-
-    @pl.when((pl.program_id(0) == 0) & (pl.program_id(1) == 0))
-    def _():
-        alog_out[...] = g_alog[...]
-        aimag_out[...] = g_aimag[...]
-        height_out[...] = g_height[...]
-        width_out[...] = g_width[...]
-        local = skip_out.shape[0]
-        dt_out[...] = rows[29:31, 0:local]
-        singles = ((skip_out, 28), (gain_out, 33), (bias_out, 34), (bout_out, 32), (scale_out, 35))
-        for out, k in singles:
-            out[...] = rows[k : k + 1, 0:local].reshape(local)
-        count = bin_out.shape[0] // local
-        bin_out[...] = jnp.concatenate(
-            [rows[36 + k : 37 + k, 0:local] for k in range(count)], axis=1
-        ).reshape(bin_out.shape)
-        win_out[...] = jnp.transpose(dw[1])
-        wout_out[...] = dw[0]
-
-
-def finish(res_own, g_own, grad_out, sums):
+def finish_kernel(parts, n_sums, *refs):
+    sums, refs = refs[:n_sums], refs[n_sums:]
+    res_ref, g_ref, result_ref, grad_ref = refs[:4]
+    n_small = (len(refs) - 11 - n_sums) // 2
+    smalls, refs = refs[4 : 4 + n_small], refs[4 + n_small :]
+    res_near, g_near, grad_near = refs[:3]
+    sums_near = refs[3 : 3 + n_sums]
+    near = refs[3 + n_sums : 3 + n_sums + n_small]
+    came, left, sums_came, smalls_left = refs[3 + n_sums + n_small :]
+    pix = g_near.shape[2]
+    in_copies, out_copies = [], []
+    for i, (a, b) in enumerate(((g_ref, g_near), (res_ref, res_near))):
+        for s in range(parts):
+            in_copies.append(pltpu.make_async_copy(a.at[s], b.at[s], came.at[i, s]))
+            in_copies[-1].start()
+        if i == 0:
+            small_in = [
+                pltpu.make_async_copy(sums[k], sums_near[k], sums_came.at[k]) for k in range(n_sums)
+            ]
+            for copy in small_in:
+                copy.start()
+
+    def put(src, dst, sem):
+        out_copies.append(pltpu.make_async_copy(src, dst, sem))
+        out_copies[-1].start()
+
+    for s in range(parts):
+        in_copies[s].wait()
+        grad_near[s] = g_near[s].astype(F32)
+        put(grad_near.at[s], grad_ref.at[:, pl.ds(s * pix, pix)], left.at[0, s])
+        if s == 0:
+            for copy in small_in:
+                copy.wait()
+            dw, g_alog, g_aimag, g_height, g_width, rows = sums_near
+            alog, aimag, height, width, dt, skip, gain, bias, win, bin_, wout, bout, scale = near
+            for out, ref in ((alog, g_alog), (aimag, g_aimag), (height, g_height), (width, g_width)):
+                out[...] = ref[...]
+            local = skip.shape[0]
+            dt[...] = rows[29:31, 0:local]
+            for out, k in ((skip, 28), (gain, 33), (bias, 34), (bout, 32), (scale, 35)):
+                out[...] = rows[k : k + 1, 0:local].reshape(local)
+            bin_[...] = jnp.concatenate(
+                [rows[36 + k : 37 + k, 0:local] for k in range(bin_.shape[0] // local)], axis=1
+            ).reshape(bin_.shape)
+            win[...] = jnp.transpose(dw[1])
+            wout[...] = dw[0]
+            for k in range(n_small):
+                put(near[k], smalls[k], smalls_left.at[k])
+    for s in range(parts):
+        in_copies[parts + s].wait()
+        put(res_near.at[s], result_ref.at[:, pl.ds(s * pix, pix)], left.at[1, s])
+    for copy in out_copies:
+        copy.wait()
+
+
+def finish(res_own, g_own, sums):
     parts, local, pix = g_own.shape
     dw, g_alog, _, g_height, _, _ = sums
-    part = pl.BlockSpec((1, GROUP, pix), lambda s, q: (s, q, 0))
-    tile = pl.BlockSpec((GROUP, pix), lambda s, q: (q, s))
-
-    def whole(a):
-        return pl.BlockSpec(a.shape, lambda s, q: (0,) * len(a.shape))
-
+    hbm = pl.BlockSpec(memory_space=pl.ANY)
+    dma = pltpu.SemaphoreType.DMA
     shape = jax.ShapeDtypeStruct
-    line = shape((local,), F32)
+    line = (local,)
     small = (
-        g_alog,
-        g_alog,
-        g_height,
-        g_height,
-        shape((2, local), F32),
+        g_alog.shape,
+        g_alog.shape,
+        g_height.shape,
+        g_height.shape,
+        (2, local),
         line,
         line,
         line,
-        shape((dw.shape[2], dw.shape[1]), F32),
-        shape((dw.shape[1],), F32),
-        shape(dw.shape[1:], F32),
+        (dw.shape[2], dw.shape[1]),
+        (dw.shape[1],),
+        dw.shape[1:],
         line,
         line,
     )
-    small = tuple(shape(a.shape, F32) for a in small)
     return pl.pallas_call(
-        finish_kernel,
-        grid=(parts, local // GROUP),
-        out_shape=(shape(grad_out.shape, BF16), shape(grad_out.shape, F32)) + small,
-        in_specs=[part, part, tile] + [whole(a) for a in sums],
-        out_specs=(tile, tile) + tuple(whole(a) for a in small),
+        functools.partial(finish_kernel, parts, len(sums)),
+        out_shape=(shape((local, parts * pix), BF16), shape((local, parts * pix), F32))
+        + tuple(shape(a, F32) for a in small),
+        in_specs=[hbm] * (2 + len(sums)),
+        out_specs=(hbm,) * (2 + len(small)),
+        scratch_shapes=[
+            pltpu.VMEM(g_own.shape, BF16),
+            pltpu.VMEM(g_own.shape, BF16),
+            pltpu.VMEM(g_own.shape, F32),
+        ]
+        + [pltpu.VMEM(a.shape, F32) for a in sums]
+        + [pltpu.VMEM(a, F32) for a in small]
+        + [dma((2, parts)), dma((2, parts)), dma((len(sums),)), dma((len(small),))],
         compiler_params=pltpu.CompilerParams(vmem_limit_bytes=VMEM),
         name="finish",
-    )(res_own, g_own, grad_out, *sums)
+    )(*sums, res_own, g_own)
 
 
 def per_device(
@@ -872,7 +949,7 @@
     if dp_size > groups:
         teams = [[r + groups * g for g in range(dp_size // groups)] for r in range(groups)]
         sums = lax.psum(sums, "dp", axis_index_groups=teams)
-    done = finish(out[0], out[1], grad_out, sums)
+    done = finish(out[0], out[1], sums)
     return (
         done[0],
         done[1],

time: 456 us -> 447 us (0.980)
  Pallas kernels: 454 us -> 446 us
    pallas_call x1, Pallas kernels: 15.5 us -> 9.87 us  [finish(): pl.pallas_call(functools.partial(finish_kernel, parts, len(sums)), out_sh...]
where the time goes in v4:
time: 447 us
  Pallas kernels  446 us (100%)
    pallas_call x1, Pallas kernels, block(): pl.pallas_call(functools.partial(block_kernel, parts, groups), out_shape=...  436 us
    pallas_call x1, Pallas kernels, finish(): pl.pallas_call(functools.partial(finish_kernel, parts, len(sums)), out_sh...  9.87 us

profile of v4, /device:TPU:24, one launch (start us, length us, event | category | flops | bytes accessed | tf_op | source)
XLA Modules:
  0.0 446.8 jit_solution(5757178535848902197)
XLA Ops:
  0.7 436.1 %block.1 = (bf16[4,96,6272]{2,1,0:T(8,128)(2,1)}, bf16[4,96,6272]{2,1,0:T(8,128)(2,1)}, f32[2,384,384]{2,1,0:T(8,128)}, f32[64,96]{1,0:T(8,128)}, f32[64,96]{1,0...) custom-call(bf16[96,25088]{1,0:T(8,128)(2,1)} %x.1, ...), custom_call_target="tpu_custom_call" | custom-call | tf_op jit(solution)/shard_map/block/pallas_call | solution.py:796
  436.8 9.9 %finish.1 = (bf16[96,25088]{1,0:T(8,128)(2,1)}, f32[96,25088]{1,0:T(8,128)}, f32[64,96]{1,0:T(8,128)}, f32[64,96]{1,0:T(8,128)}, f32[2,64,96]{2,1,0:T(8,128)}, /...) custom-call(f32[2,384,384]{2,1,0:T(8,128)} %get-tuple-element.38.ref, ...), custom_call_target="tpu_custom_call" | custom-call | tf_op jit(solution)/shard_map/finish/pallas_call | solution.py:886

commit v5 on v4

--- a/solution.py
+++ b/solution.py
@@ -282,6 +282,7 @@
     dw_sum,
     dw_low,
     dw_tensor,
+    dw_pass,
     dw_done,
     bin_acc,
     vec,
@@ -289,11 +290,14 @@
     pack_peer,
     pack_sum,
     pack_tensor,
+    pack_pass,
     send,
     recv,
     own,
     hop_send,
     hop_recv,
+    leg_send,
+    leg_recv,
     hid_sem,
     slope_sem,
     go_sem,
@@ -632,7 +636,7 @@
     def _(q):
         mix_bwd(q, x_all, rows, grow, kern, mask, inner, mid, mixed, gkern)
 
-        @pl.when(q + 1 < local // GROUP)
+        @pl.when(q == 0)
         def _():
             for copy in gx_copies(q):
                 copy.start()
@@ -674,20 +678,71 @@
     terms = [dw[:, :, i * slab : (i + 1) * slab, :] for i in range(groups)]
     dw_sum[...] = sum(terms[1:], terms[0])
     dw_low[...] = dw_sum[...].astype(BF16)
-    dw_copies = [remote(dw_low.at[:, t], dw_tensor.at[me], p) for t, p in zip(others, across)]
+
+    def leg(kind, way, src, slot, peer):
+        return pltpu.make_async_remote_copy(
+            src_ref=src,
+            dst_ref=(dw_tensor, pack_tensor)[kind].at[slot],
+            send_sem=leg_send.at[kind, way],
+            recv_sem=leg_recv.at[kind, slot],
+            device_id=peer,
+            device_id_type=MESH,
+        )
+
+    def term(kind, t):
+        return pack_sum.at[t] if kind else dw_low.at[:, t]
+
+    def to_partner(kind):
+        return leg(kind, 0, term(kind, partner["tensor"]), 0, partner)
+
+    def to_inner(kind, k):
+        return leg(kind, 1 + k, term(kind, other_half + k), 2 + k, partner)
+
+    def crossing(kind, k):
+        src = (dw_pass, pack_pass)[kind].at[k]
+        return leg(kind, 3 + k, src, 1, {"tensor": other_half + k})
+
+    def start_leg(kind):
+        to_partner(kind).start()
+
+        @pl.when(jnp.logical_not(is_inner))
+        def _():
+            for k in range(2):
+                to_inner(kind, k).start()
+
+    start_leg(0)
     arrived(pack_copies)
     pack_sum[...] = sum((pack_peer[i] for i in range(1, groups)), pack_peer[0])
-    pack_tensor[me] = pack_sum[me]
-    pack_copies = [remote(pack_sum.at[t], pack_tensor.at[me], p) for t, p in zip(others, across)]
-    for copy in gx_copies(local // GROUP - 1):
+    start_leg(1)
+    for copy in gx_copies(1):
         copy.start()
 
-    arrived(dw_copies)
-    dw_done[...] = sum((dw_tensor[t].astype(F32) for t in others), dw_sum[:, me])
+    @pl.when(is_inner)
+    def _():
+        for kind in range(2):
+            for k in range(2):
+                to_inner(kind, k).wait_recv()
+        for k in range(2):
+            dw_pass[k] = (dw_sum[:, other_half + k] + dw_tensor[2 + k].astype(F32)).astype(BF16)
+            pack_pass[k] = pack_sum[other_half + k] + pack_tensor[2 + k]
+        for kind in range(2):
+            for k in range(2):
+                crossing(kind, k).start()
+
+    for q in range(2, local // GROUP):
+        for copy in gx_copies(q):
+            copy.start()
+
+    def received(kind):
+        to_partner(kind).wait_recv()
+        crossing(kind, 0).wait_recv()
+
+    received(0)
+    dw_done[...] = dw_sum[:, me] + dw_tensor[0].astype(F32) + dw_tensor[1].astype(F32)
     dw_near = near(dw_done, dw_own.at[:, my_slab, :])
     dw_copies = [remote(dw_done, dw_own.at[:, my_slab, :], p) for p in beside]
-    arrived(pack_copies)
-    total = sum((pack_tensor[i] for i in range(1, parts)), pack_tensor[0])
+    received(1)
+    total = pack_sum[me] + pack_tensor[0] + pack_tensor[1]
     gdt = lag_grads(total, steps, a_log, a_imag, coefs, g_alog, g_aimag, [g_height, g_width])
     row_own[...] = total
     for j in range(2):
@@ -704,12 +759,23 @@
 
     for copy in sent + first_hops:
         copy.wait_send()
+
+    for kind in range(2):
+        to_partner(kind).wait_send()
 
     @pl.when(is_inner)
     def _():
         for k in range(2):
             for copy in handed_on(k):
                 copy.wait_send()
+            for kind in range(2):
+                crossing(kind, k).wait_send()
+
+    @pl.when(jnp.logical_not(is_inner))
+    def _():
+        for k in range(2):
+            for kind in range(2):
+                to_inner(kind, k).wait_send()
 
 
 def block(parts, groups, args):
@@ -742,7 +808,7 @@
         (shape((parts, local, pix), BF16), hbm),
         (shape((2, parts, shard, width), F32), hbm),
     ]
-    remotes = 5 * (parts - 1) + 5 * (groups - 1)
+    remotes = 4 * (parts - 1) + 5 * (groups - 1)
     dma = pltpu.SemaphoreType.DMA
     scratch = [
         pltpu.VMEM((parts, local, pix), BF16),
@@ -772,19 +838,23 @@
         pltpu.VMEM((2, parts, shard, width), F32),
         pltpu.VMEM((2, parts, slab, width), F32),
         pltpu.VMEM((2, parts, slab, width), BF16),
-        pltpu.VMEM((parts, 2, slab, width), BF16),
+        pltpu.VMEM((4, 2, slab, width), BF16),
+        pltpu.VMEM((2, 2, slab, width), BF16),
         pltpu.VMEM((2, slab, width), F32),
         pltpu.VMEM((ff, LANES), F32),
         pltpu.VMEM((4, width, LANES), F32),
         pltpu.VMEM((parts, 40, LANES), F32),
         pltpu.VMEM((groups, parts, 40, LANES), F32),
         pltpu.VMEM((parts, 40, LANES), F32),
-        pltpu.VMEM((parts, 40, LANES), F32),
+        pltpu.VMEM((4, 40, LANES), F32),
+        pltpu.VMEM((2, 40, LANES), F32),
         dma((remotes,)),
         dma((remotes,)),
         dma((10,)),
         dma((4, 3)),
         dma((3, 3)),
+        dma((2, 5)),
+        dma((2, 4)),
         dma((parts,)),
         dma((parts,)),
         dma((parts,)),

time: 447 us -> 443 us (level)
  no operation moved by 1% of the time
where the time goes in v5:
time: 443 us
  Pallas kernels  442 us (100%)
    pallas_call x1, Pallas kernels, block(): pl.pallas_call(functools.partial(block_kernel, parts, groups), out_shape=...  432 us
    pallas_call x1, Pallas kernels, finish(): pl.pallas_call(functools.partial(finish_kernel, parts, len(sums)), out_sh...  9.87 us

profile of v5, /device:TPU:24, one launch (start us, length us, event | category | flops | bytes accessed | tf_op | source)
XLA Modules:
  0.0 443.0 jit_solution(2943838778961812707)
XLA Ops:
  0.7 432.3 %block.1 = (bf16[4,96,6272]{2,1,0:T(8,128)(2,1)}, bf16[4,96,6272]{2,1,0:T(8,128)(2,1)}, f32[2,384,384]{2,1,0:T(8,128)}, f32[64,96]{1,0:T(8,128)}, f32[64,96]{1,0...) custom-call(bf16[96,25088]{1,0:T(8,128)(2,1)} %x.1, ...), custom_call_target="tpu_custom_call" | custom-call | tf_op jit(solution)/shard_map/block/pallas_call | solution.py:866
  433.0 9.9 %finish.1 = (bf16[96,25088]{1,0:T(8,128)(2,1)}, f32[96,25088]{1,0:T(8,128)}, f32[64,96]{1,0:T(8,128)}, f32[64,96]{1,0:T(8,128)}, f32[2,64,96]{2,1,0:T(8,128)}, /...) custom-call(f32[2,384,384]{2,1,0:T(8,128)} %get-tuple-element.38.ref, ...), custom_call_target="tpu_custom_call" | custom-call | tf_op jit(solution)/shard_map/finish/pallas_call | solution.py:956

commit v6 on v5

--- a/solution.py
+++ b/solution.py
@@ -17,7 +17,7 @@
 EPS = 1e-06
 GELU_C = 0.7978845608028654
 GELU_A = 0.044715
-VMEM = 63 << 20
+VMEM = 53 << 20
 MESH = pl.DeviceIdType.MESH
 
 
@@ -256,7 +256,6 @@
     dw_peer,
     x_all,
     mixed,
-    res_near,
     rows,
     grow,
     inner,
@@ -271,13 +270,12 @@
     square,
     turned,
     win,
-    win_t,
     wout,
     wout_t,
     hid,
     slope,
     gp,
-    go_near,
+    chunk_near,
     dw,
     dw_sum,
     dw_low,
@@ -308,7 +306,8 @@
 ):
     local, pix = x_all.shape[1], x_all.shape[2]
     width = local * parts
-    ff = win_t.shape[0]
+    ff = gp.shape[0]
+    win_t = gp.at[:, 0:width]
     shard = ff // parts
     slab = shard // groups
     chunks = pix // STEP
@@ -491,7 +490,7 @@
         lanes = pl.ds(pl.multiple_of(j * STEP, LANES), STEP)
         pairs = [(t, res) for t in others] + [(me, res_own)]
         return [
-            pltpu.make_async_copy(res_near.at[t], ref.at[t, :, lanes], res_sem.at[i])
+            pltpu.make_async_copy(chunk_near.at[t], ref.at[t, :, lanes], res_sem.at[i])
             for i, (t, ref) in enumerate(pairs)
         ]
 
@@ -504,20 +503,20 @@
         off = pl.multiple_of(j * STEP, LANES)
         _, _, low = low_of(off)
         for t in range(parts):
-            sl = pl.ds(t * shard, shard)
-            pre = nn(win_t[sl, :], low) + bin_col[sl, 0:1]
-            square_pre = pre * pre
-            th = jnp.tanh(pre * (GELU_C + (GELU_C * GELU_A) * square_pre))
-            half = 0.5 * th + 0.5
-            inner_slope = GELU_C + (3 * GELU_C * GELU_A) * square_pre
-
             @pl.when(j > 0)
             def _():
                 for copy in hid_copy(t, j, False):
                     copy.wait()
 
-            hid[sl, :] = (pre * half).astype(BF16)
-            slope[sl, :] = (half + pre * (0.5 - 0.5 * th * th) * inner_slope).astype(BF16)
+            for part in range(2):
+                sl = pl.ds(t * shard + part * (shard // 2), shard // 2)
+                pre = nn(win_t[sl, :], low) + bin_col[sl, 0:1]
+                square_pre = pre * pre
+                th = jnp.tanh(pre * (GELU_C + (GELU_C * GELU_A) * square_pre))
+                half = 0.5 * th + 0.5
+                inner_slope = GELU_C + (3 * GELU_C * GELU_A) * square_pre
+                hid[sl, :] = (pre * half).astype(BF16)
+                slope[sl, :] = (half + pre * (0.5 - 0.5 * th * th) * inner_slope).astype(BF16)
             for copy in hid_copy(t, j, False):
                 copy.start()
         branch = nn(wout_t[...], hid[...]) + chan[:, 2:3]
@@ -529,7 +528,7 @@
             for copy in res_chunk(j):
                 copy.wait()
 
-        res_near[...] = out.reshape(parts, local, STEP)
+        chunk_near[...] = out.reshape(parts, local, STEP)
         for copy in res_chunk(j):
             copy.start()
 
@@ -553,7 +552,7 @@
         mine_at = pl.ds(pl.multiple_of(me * pix + off, LANES), STEP)
         sources = [(t, go_all.at[t, :, pl.ds(off, STEP)]) for t in others] + [(me, go.at[:, mine_at])]
         return [
-            pltpu.make_async_copy(src, go_near.at[t], go_sem.at[i])
+            pltpu.make_async_copy(src, chunk_near.at[t], go_sem.at[i])
             for i, (t, src) in enumerate(sources)
         ]
 
@@ -565,7 +564,7 @@
         off = pl.multiple_of(j * STEP, LANES)
         for copy in go_chunk(j):
             copy.wait()
-        grad = go_near[...].reshape(width, STEP).astype(F32)
+        grad = chunk_near[...].reshape(width, STEP).astype(F32)
         gb = (grad * chan[:, 3:4]).astype(BF16)
         vec[0] += fold(gb.astype(F32))
         vec[3] += fold(grad)
@@ -794,14 +793,14 @@
     hbm = pl.BlockSpec(memory_space=pl.ANY)
     in_specs = [hbm, hbm] + [vmem] * 10 + [hbm, vmem, hbm, vmem, vmem]
     outs = [
-        (shape((parts, local, pix), BF16), hbm),
-        (shape((parts, local, pix), BF16), hbm),
-        (shape((2, shard, width), F32), hbm),
-        (shape((states, local), F32), vmem),
-        (shape((states, local), F32), vmem),
-        (shape((2, states, local), F32), vmem),
-        (shape((2, states, local), F32), vmem),
-        (shape((40, LANES), F32), vmem),
+        (pltpu.VMEM((parts, local, pix), BF16), vmem),
+        (pltpu.VMEM((parts, local, pix), BF16), vmem),
+        (pltpu.VMEM((2, shard, width), F32), vmem),
+        (pltpu.VMEM((states, local), F32), vmem),
+        (pltpu.VMEM((states, local), F32), vmem),
+        (pltpu.VMEM((2, states, local), F32), vmem),
+        (pltpu.VMEM((2, states, local), F32), vmem),
+        (pltpu.VMEM((40, LANES), F32), vmem),
         (shape((parts, local, pix), BF16), hbm),
         (shape((ff, pix), BF16), hbm),
         (shape((ff, pix), BF16), hbm),
@@ -813,7 +812,6 @@
     scratch = [
         pltpu.VMEM((parts, local, pix), BF16),
         pltpu.VMEM((parts, local, pix), BF16),
-        pltpu.VMEM((parts, local, STEP), BF16),
         pltpu.VMEM((pix, LANES), F32),
         pltpu.VMEM((tiles, pix, LANES), F32),
         pltpu.VMEM((CROP, CROP, 8, LANES), F32),
@@ -828,7 +826,6 @@
         pltpu.VMEM((LANES, width), F32),
         pltpu.VMEM((LANES, LANES), F32),
         pltpu.VMEM((width, ff), BF16),
-        pltpu.VMEM((ff, width), BF16),
         pltpu.VMEM((parts, shard, width), BF16),
         pltpu.VMEM((width, ff), BF16),
         pltpu.VMEM((ff, STEP), BF16),
@@ -879,37 +876,25 @@
 def finish_kernel(parts, n_sums, *refs):
     sums, refs = refs[:n_sums], refs[n_sums:]
     res_ref, g_ref, result_ref, grad_ref = refs[:4]
-    n_small = (len(refs) - 11 - n_sums) // 2
+    n_small = (len(refs) - 7) // 2
     smalls, refs = refs[4 : 4 + n_small], refs[4 + n_small :]
-    res_near, g_near, grad_near = refs[:3]
-    sums_near = refs[3 : 3 + n_sums]
-    near = refs[3 + n_sums : 3 + n_sums + n_small]
-    came, left, sums_came, smalls_left = refs[3 + n_sums + n_small :]
-    pix = g_near.shape[2]
-    in_copies, out_copies = [], []
-    for i, (a, b) in enumerate(((g_ref, g_near), (res_ref, res_near))):
-        for s in range(parts):
-            in_copies.append(pltpu.make_async_copy(a.at[s], b.at[s], came.at[i, s]))
-            in_copies[-1].start()
-        if i == 0:
-            small_in = [
-                pltpu.make_async_copy(sums[k], sums_near[k], sums_came.at[k]) for k in range(n_sums)
-            ]
-            for copy in small_in:
-                copy.start()
+    grad_near = refs[0]
+    near = refs[1 : 1 + n_small]
+    left, smalls_left = refs[1 + n_small :]
+    pix = g_ref.shape[2]
+    out_copies = []
 
     def put(src, dst, sem):
         out_copies.append(pltpu.make_async_copy(src, dst, sem))
         out_copies[-1].start()
 
     for s in range(parts):
-        in_copies[s].wait()
-        grad_near[s] = g_near[s].astype(F32)
+        put(res_ref.at[s], result_ref.at[:, pl.ds(s * pix, pix)], left.at[1, s])
+    for s in range(parts):
+        grad_near[s] = g_ref[s].astype(F32)
         put(grad_near.at[s], grad_ref.at[:, pl.ds(s * pix, pix)], left.at[0, s])
         if s == 0:
-            for copy in small_in:
-                copy.wait()
-            dw, g_alog, g_aimag, g_height, g_width, rows = sums_near
+            dw, g_alog, g_aimag, g_height, g_width, rows = sums
             alog, aimag, height, width, dt, skip, gain, bias, win, bin_, wout, bout, scale = near
             for out, ref in ((alog, g_alog), (aimag, g_aimag), (height, g_height), (width, g_width)):
                 out[...] = ref[...]
@@ -924,9 +909,6 @@
             wout[...] = dw[0]
             for k in range(n_small):
                 put(near[k], smalls[k], smalls_left.at[k])
-    for s in range(parts):
-        in_copies[parts + s].wait()
-        put(res_near.at[s], result_ref.at[:, pl.ds(s * pix, pix)], left.at[1, s])
     for copy in out_copies:
         copy.wait()
 
@@ -935,6 +917,7 @@
     parts, local, pix = g_own.shape
     dw, g_alog, _, g_height, _, _ = sums
     hbm = pl.BlockSpec(memory_space=pl.ANY)
+    vmem = pl.BlockSpec(memory_space=pltpu.VMEM)
     dma = pltpu.SemaphoreType.DMA
     shape = jax.ShapeDtypeStruct
     line = (local,)
@@ -957,17 +940,14 @@
         functools.partial(finish_kernel, parts, len(sums)),
         out_shape=(shape((local, parts * pix), BF16), shape((local, parts * pix), F32))
         + tuple(shape(a, F32) for a in small),
-        in_specs=[hbm] * (2 + len(sums)),
+        in_specs=[vmem] * (len(sums) + 2),
         out_specs=(hbm,) * (2 + len(small)),
         scratch_shapes=[
-            pltpu.VMEM(g_own.shape, BF16),
-            pltpu.VMEM(g_own.shape, BF16),
             pltpu.VMEM(g_own.shape, F32),
         ]
-        + [pltpu.VMEM(a.shape, F32) for a in sums]
         + [pltpu.VMEM(a, F32) for a in small]
-        + [dma((2, parts)), dma((2, parts)), dma((len(sums),)), dma((len(small),))],
-        compiler_params=pltpu.CompilerParams(vmem_limit_bytes=VMEM),
+        + [dma((2, parts)), dma((len(small),))],
+        compiler_params=pltpu.CompilerParams(vmem_limit_bytes=24 << 20),
         name="finish",
     )(*sums, res_own, g_own)
 

time: 443 us -> 438 us (0.989)
  Pallas kernels: 442 us -> 437 us
where the time goes in v6:
time: 438 us
  Pallas kernels  437 us (100%)
    pallas_call x1, Pallas kernels, block(): pl.pallas_call(functools.partial(block_kernel, parts, groups), out_shape=...  431 us

profile of v6, /device:TPU:24, one launch (start us, length us, event | category | flops | bytes accessed | tf_op | source)
XLA Modules:
  0.0 438.1 jit_solution(658232407091861274)
XLA Ops:
  0.7 431.5 %block.1 = (bf16[4,96,6272]{2,1,0:T(8,128)(2,1)S(1)}, bf16[4,96,6272]{2,1,0:T(8,128)(2,1)S(1)}, f32[2,384,384]{2,1,0:T(8,128)S(1)}, f32[64,96]{1,0:T(8,128)S(1)}...) custom-call(bf16[96,25088]{1,0:T(8,128)(2,1)} %x.1, ...), custom_call_target="tpu_custom_call" | custom-call | tf_op jit(solution)/shard_map/block/pallas_call | solution.py:863
  432.1 5.8 %finish.1 = (bf16[96,25088]{1,0:T(8,128)(2,1)}, f32[96,25088]{1,0:T(8,128)}, f32[64,96]{1,0:T(8,128)}, f32[64,96]{1,0:T(8,128)}, f32[2,64,96]{2,1,0:T(8,128)}, /...) custom-call(f32[2,384,384]{2,1,0:T(8,128)S(1)} %get-tuple-element.38, ...), custom_call_target="tpu_custom_call" | custom-call | tf_op jit(solution)/shard_map/finish/pallas_call | solution.py:939

commit v7 on v6

--- a/solution.py
+++ b/solution.py
@@ -292,6 +292,8 @@
     send,
     recv,
     own,
+    x_send,
+    x_recv,
     hop_send,
     hop_recv,
     leg_send,
@@ -412,6 +414,21 @@
         found = pieces(other_half + k)
         return [hop(i, 1 + k, found[i], partner, 2 + k) for i in range(3)]
 
+    def x_copy(k, came=False):
+        peer = partner["tensor"] if k == 2 else other_half + k
+        slot = k if k == 2 or came else lax.rem(me, 2)
+        return pltpu.make_async_remote_copy(
+            src_ref=pixels(x, peer),
+            dst_ref=x_all.at[peer if came else me],
+            send_sem=x_send.at[k],
+            recv_sem=x_recv.at[slot],
+            device_id={"tensor": peer},
+            device_id_type=MESH,
+        )
+
+    for k in range(2):
+        x_copy(k).start()
+
     @pl.when(is_inner)
     def _():
         for k in range(2):
@@ -420,7 +437,7 @@
             for copy in handed_on(k):
                 copy.start()
 
-    x_copies = to_owner(x, x_all)
+    x_copy(2).start()
     x_near = near(pixels(x, me), x_all.at[me])
 
     @pl.when(jnp.logical_not(is_inner))
@@ -467,7 +484,8 @@
         win_t[cols, :] = jnp.transpose(win[:, cols].astype(F32)).astype(BF16)
         wout_t[:, cols] = jnp.transpose(wout[t].astype(F32)).astype(BF16)
 
-    arrived(x_copies)
+    for k in range(3):
+        x_copy(k, came=True).wait_recv()
     x_near.wait()
     go_copies = to_owner(go, go_all)
 
@@ -756,7 +774,7 @@
         for copy in gx_copies(q):
             copy.wait()
 
-    for copy in sent + first_hops:
+    for copy in sent + first_hops + [x_copy(k) for k in range(3)]:
         copy.wait_send()
 
     for kind in range(2):
@@ -848,6 +866,8 @@
         dma((remotes,)),
         dma((remotes,)),
         dma((10,)),
+        dma((3,)),
+        dma((3,)),
         dma((4, 3)),
         dma((3, 3)),
         dma((2, 5)),

time: 438 us -> 437 us (level)
  no operation moved by 1% of the time
where the time goes in v7:
time: 437 us
  Pallas kernels  436 us (100%)
    pallas_call x1, Pallas kernels, block(): pl.pallas_call(functools.partial(block_kernel, parts, groups), out_shape=...  430 us

profile of v7, /device:TPU:24, one launch (start us, length us, event | category | flops | bytes accessed | tf_op | source)
XLA Modules:
  0.0 437.0 jit_solution(1704673228540948588)
XLA Ops:
  0.7 430.4 %block.1 = (bf16[4,96,6272]{2,1,0:T(8,128)(2,1)S(1)}, bf16[4,96,6272]{2,1,0:T(8,128)(2,1)S(1)}, f32[2,384,384]{2,1,0:T(8,128)S(1)}, f32[64,96]{1,0:T(8,128)S(1)}...) custom-call(bf16[96,25088]{1,0:T(8,128)(2,1)} %x.1, ...), custom_call_target="tpu_custom_call" | custom-call | tf_op jit(solution)/shard_map/block/pallas_call | solution.py:883
  431.0 5.8 %finish.1 = (bf16[96,25088]{1,0:T(8,128)(2,1)}, f32[96,25088]{1,0:T(8,128)}, f32[64,96]{1,0:T(8,128)}, f32[64,96]{1,0:T(8,128)}, f32[2,64,96]{2,1,0:T(8,128)}, /...) custom-call(f32[2,384,384]{2,1,0:T(8,128)S(1)} %get-tuple-element.38, ...), custom_call_target="tpu_custom_call" | custom-call | tf_op jit(solution)/shard_map/finish/pallas_call | solution.py:959

commit v8 on v7

--- a/solution.py
+++ b/solution.py
@@ -323,6 +323,14 @@
     barrier = pltpu.get_barrier_semaphore()
     for peer in across + beside:
         pl.semaphore_signal(barrier, inc=1, device_id=peer, device_id_type=MESH)
+    steps = [jnp.exp(log_dt[j : j + 1, :]) for j in range(2)]
+    coefs = [c_height, c_width]
+    small_mine[...] = jnp.zeros_like(small_mine)
+    lag_kernels(steps, a_log, a_imag, coefs, small_mine)
+    small_mine[2 * CROP : 2 * CROP + 1, 0:local] = skip_gain[...].reshape(1, local)
+    biases = b_in[...].reshape(1, shard)
+    for j in range(shard // LANES):
+        small_mine[32 + j : 33 + j, :] = biases[:, j * LANES : (j + 1) * LANES]
     pl.semaphore_wait(barrier, len(across) + len(beside))
 
     count = [0, 0]
@@ -364,8 +372,6 @@
         return [remote(pixels(ref, p["tensor"]), out.at[me], p) for p in across]
 
     my_slab = pl.ds(pl.multiple_of(mine * slab, slab), slab)
-    steps = [jnp.exp(log_dt[j : j + 1, :]) for j in range(2)]
-    coefs = [c_height, c_width]
 
     partner = {"tensor": me + 1 - 2 * lax.rem(me, 2)}
     inner_device = {"tensor": jnp.where(me < 2, 2, 1)}
@@ -395,13 +401,6 @@
     first_hops = []
     slabs = [w_in.at[my_slab, :], w_out.at[my_slab, :], small_mine]
     for i in range(3):
-        if i == 2:
-            small_mine[...] = jnp.zeros_like(small_mine)
-            lag_kernels(steps, a_log, a_imag, coefs, small_mine)
-            small_mine[2 * CROP : 2 * CROP + 1, 0:local] = skip_gain[...].reshape(1, local)
-            biases = b_in[...].reshape(1, shard)
-            for j in range(shard // LANES):
-                small_mine[32 + j : 33 + j, :] = biases[:, j * LANES : (j + 1) * LANES]
         pair = (slabs[i], pieces(me)[i][1])
         first_hops.append(hop(i, 0, pair, partner, 0))
         first_hops.append(hop(i, 1 + lax.rem(me, 2), pair, inner_device, 1))

time: 437 us -> 437 us (level)
  no operation moved by 1% of the time
where the time goes in v8:
time: 437 us
  Pallas kernels  436 us (100%)
    pallas_call x1, Pallas kernels, block(): pl.pallas_call(functools.partial(block_kernel, parts, groups), out_shape=...  430 us

profile of v8, /device:TPU:24, one launch (start us, length us, event | category | flops | bytes accessed | tf_op | source)
XLA Modules:
  0.0 437.0 jit_solution(13125624391412798589)
XLA Ops:
  0.7 430.4 %block.1 = (bf16[4,96,6272]{2,1,0:T(8,128)(2,1)S(1)}, bf16[4,96,6272]{2,1,0:T(8,128)(2,1)S(1)}, f32[2,384,384]{2,1,0:T(8,128)S(1)}, f32[64,96]{1,0:T(8,128)S(1)}...) custom-call(bf16[96,25088]{1,0:T(8,128)(2,1)} %x.1, ...), custom_call_target="tpu_custom_call" | custom-call | tf_op jit(solution)/shard_map/block/pallas_call | solution.py:882
  431.0 5.8 %finish.1 = (bf16[96,25088]{1,0:T(8,128)(2,1)}, f32[96,25088]{1,0:T(8,128)}, f32[64,96]{1,0:T(8,128)}, f32[64,96]{1,0:T(8,128)}, f32[2,64,96]{2,1,0:T(8,128)}, /...) custom-call(f32[2,384,384]{2,1,0:T(8,128)S(1)} %get-tuple-element.38, ...), custom_call_target="tpu_custom_call" | custom-call | tf_op jit(solution)/shard_map/finish/pallas_call | solution.py:958
